TPU v7x, 512 devices: a whole 4x4x16 slice. The times are simulated.
512 devices in a mesh: space: 32 (over z, x_lo), chan: 16 (over x_hi, y, core).
Axes of the slice: x: 4 (x_hi: 2, x_lo: 2; x = x_hi * 2 + x_lo), y: 4, z: 16, core: 2. Of those that a mesh axis runs over, the one named last changes fastest.
Arguments:
- volume: bfloat16 [64, 256, 8, 128], P('space', 'chan'), may hold values from -6 to 6
- kernel: bfloat16 [27, 256, 256], P(None, 'chan'), may hold values from -0.078125 to 0.078125
- cotangent: bfloat16 [64, 256, 8, 128], P('space', 'chan'), may hold values from -6 to 6
Outputs:
- output_map: bfloat16 [64, 256, 8, 128], P('space', 'chan')
- input_grad: bfloat16 [64, 256, 8, 128], P('space', 'chan')
- kernel_grad: float32 [27, 256, 256], P(None, 'chan')
All inputs are finite; a program needn't handle non-finite values.
Results may differ from a plain program's by a relative error of at most 0.001.
Values may be sent and summed in bfloat16 or wider, within the bound.
A program may use at most 128 MiB of HBM per device.

v0:
```python
import math

import jax
import jax.numpy as jnp
from jax import lax
from jax.sharding import PartitionSpec as P


def with_halo(block, sides, width):
    for axis, dim in sides:
        count = lax.axis_size(axis)
        forward = [(i, i + 1) for i in range(count - 1)]
        backward = [(target, source) for source, target in forward]
        low = lax.ppermute(
            lax.slice_in_dim(block, block.shape[dim] - width, None, axis=dim), axis, forward
        )
        high = lax.ppermute(lax.slice_in_dim(block, 0, width, axis=dim), axis, backward)
        block = jnp.concatenate([low, block, high], axis=dim)
    return block


def plane_stack(piece, height, width, flipped):
    cells = height * width
    padded = jnp.pad(piece, ((0, 0), (0, 0), (width + 1, width + 1)))
    column = lax.broadcasted_iota(jnp.int32, (1, 1, cells), 2) % width
    windows = []
    for row_step in range(3):
        for col_step in range(3):
            row_from = 2 - row_step if flipped else row_step
            col_from = 2 - col_step if flipped else col_step
            offset = width + 1 + (row_from - 1) * width + (col_from - 1)
            shifted = padded[:, :, offset : offset + cells]
            target = column + (col_from - 1)
            inside = ((target >= 0) & (target < width)).astype(piece.dtype)
            windows.append(shifted * inside)
    return jnp.concatenate(windows, axis=1)


def on_device(volume, kernel, cotangent):
    depth, chans_local, height, width = volume.shape
    filters_local = cotangent.shape[1]
    cells = height * width
    scale_factor = 1.0 / math.sqrt(depth * lax.axis_size("space") * height * width)
    volume_flat = volume.reshape(depth, chans_local, cells)
    grad_flat = cotangent.reshape(depth, filters_local, cells)
    columns = lax.all_to_all(kernel, "chan", split_axis=2, concat_axis=1, tiled=True)
    init_output = jnp.zeros((depth, filters_local, cells), jnp.float32)
    init_input = jnp.zeros((depth, chans_local, cells), jnp.float32)
    rims = with_halo(volume_flat, (("space", 0),), 1)
    piece = lax.all_gather(rims, "chan", axis=1, tiled=True)
    output_acc = init_output
    count = piece.shape[1]
    stacked = plane_stack(piece, height, width, False)
    grads = []
    for depth_step in range(3):
        window = stacked[depth_step : depth_step + depth]
        taps = kernel[9 * depth_step : 9 * depth_step + 9]
        weights = jnp.transpose(taps, (1, 0, 2)).reshape(filters_local, 9 * count)
        output_acc = output_acc + jnp.einsum(
            "fj,zjp->zfp", weights, window, preferred_element_type=jnp.float32
        )
        term = jnp.einsum("zfp,zjp->fj", grad_flat, window, preferred_element_type=jnp.float32)
        grads.append(jnp.transpose(term.reshape(filters_local, 9, count), (1, 0, 2)))
    kernel_acc = jnp.concatenate(grads, axis=0)
    output_acc, kernel_acc = (output_acc, kernel_acc)
    grad_ext = with_halo(grad_flat, (("space", 0),), 1)
    total = init_input
    piece = lax.all_gather(grad_ext, "chan", axis=1, tiled=True)
    count = piece.shape[1]
    stacked = plane_stack(piece, height, width, True)
    for depth_step in range(3):
        window = stacked[2 - depth_step : 2 - depth_step + depth]
        taps = columns[9 * depth_step : 9 * depth_step + 9]
        weights = jnp.transpose(taps, (2, 0, 1)).reshape(chans_local, 9 * count)
        total = total + jnp.einsum(
            "kj,zjp->zkp", weights, window, preferred_element_type=jnp.float32
        )
    kernel_grad = lax.psum(kernel_acc, "space") * scale_factor
    output_map = output_acc.astype(jnp.bfloat16).reshape(depth, filters_local, height, width)
    input_grad = total.astype(jnp.bfloat16).reshape(depth, chans_local, height, width)
    return (output_map, input_grad, kernel_grad)


def solution(mesh):
    return jax.shard_map(
        on_device,
        mesh=mesh,
        in_specs=(
            P("space", "chan", None, None),
            P(None, "chan", None),
            P("space", "chan", None, None),
        ),
        out_specs=(
            P("space", "chan", None, None),
            P("space", "chan", None, None),
            P(None, "chan", None),
        ),
        check_vma=False,
    )
```

profile of v0, /device:TPU:8, one launch (start us, length us, event | category | flops | bytes accessed | tf_op | source)
XLA Modules:
  0.0 456.4 jit_solution(4387820770311451748)
XLA Ops:
  7.2 0.8 fusion.80
  8.1 3.4 collective-permute-start.2
  11.5 1.3 collective-permute-start.3
  12.8 0.9 reshape.102
  13.7 3.6 collective-permute-done.3
  18.0 0.8 fusion.81
  18.9 4.7 %collective-permute-start = (bf16[1,16,1024]{2,1,0:T(8,128)(2,1)S(1)}, bf16[1,16,1024]{2,1,0:T(8,128)(2,1)S(1)}, u32[]{:S(2)}, u32[]{:S(2)}) collective-permute-start(bf16[1,16,1024]{2,1,0:T(8,128)(2,1)S(1)} %slice.120), channel_id=1, source_target_pairs={{0,16},{16,32},{32,48},{48,64},{64,80},{80,96},{96,112},{112,128},... | collective-permute-start | bytes 98312 | tf_op jit(solution)/shard_map/ppermute | solution.py:14
  23.6 1.3 collective-permute-start.1
  24.9 0.9 reshape.97
  25.8 3.6 collective-permute-done.1
  30.1 2.0 copy.40
  32.1 2.5 reshape.125
  34.6 7.4 %all-to-all-start = ((bf16[16,2,3456]{2,1,0:T(2,128)(2,1)}), bf16[16,2,3456]{2,1,0:T(2,128)(2,1)S(1)}, u32[]{:S(2)}, u32[]{:S(2)}) async-start(bf16[16,2,3456]{2,1,0:T(2,128)(2,1)} %reshape.125), calls=%async_computation | async-start | bytes 442368 | tf_op jit(solution)/shard_map/all_to_all | solution.py:46
  44.3 5.4 %all-to-all-done = bf16[16,2,3456]{2,1,0:T(2,128)(2,1)S(1)} async-done(((bf16[16,2,3456]{2,1,0:T(2,128)(2,1)}), bf16[16,2,3456]{2,1,0:T(2,128)(2,1)S(1)}, u32[]{:S(2)}, u32[]{:S(2)}) %all-to-all-start) | async-done | bytes 221216 | tf_op jit(solution)/shard_map/all_to_all | solution.py:46
  49.6 2.7 reshape.126
  52.3 3.9 copy.49
  56.7 0.8 copy.46
  58.1 0.8 copy.44
  59.6 0.8 copy.42
  61.0 26.7 %all-gather.5.cloned.1.call-done = bf16[4,256,1024]{2,1,0:T(8,128)(2,1)} async-done(((bf16[4,16,1024]{2,1,0:T(8,128)(2,1)}), bf16[4,256,1024]{2,1,0:T(8,128)(2,1)}) %all-gather.5.cloned.1.call-update) | async-done | bytes 2097168 | tf_op jit(solution)/shard_map/all_gather | solution.py:68
  87.7 3.8 fusion.29
  91.5 1.9 fusion.31
  93.3 2.6 fusion.33
  95.9 2.6 fusion.35
  98.5 1.9 multiply_dynamic-update-slice_fusion
  100.4 52.5 %all-gather.3.cloned.1.call-done = bf16[4,256,1024]{2,1,0:T(8,128)(2,1)} async-done(((bf16[4,16,1024]{2,1,0:T(8,128)(2,1)}), bf16[4,256,1024]{2,1,0:T(8,128)(2,1)}) %all-gather.3.cloned.1.call-update) | async-done | bytes 2097168 | tf_op jit(solution)/shard_map/all_gather | solution.py:50
  152.9 4.5 fusion.37
  157.3 2.7 fusion.39
  160.0 2.5 fusion.41
  162.4 1.3 fusion.17
  163.8 3.9 fusion.43
  168.3 1.2 fusion.21
  169.6 1.2 fusion.23
  171.4 1.1 fusion.27
  172.5 2.5 convolution_bitcast_fusion.2
  175.0 2.8 convolution_bitcast_fusion.1
  177.8 1.1 copy-done
  178.9 2.5 convolution_bitcast_fusion
  181.5 0.9 pad_maximum_fusion
  182.4 5.0 %fusion = f32[2,1024,16]{1,2,0:T(8,128)S(1)} fusion(bf16[16,2304,1]{1,0,2:T(8,128)(2,1)S(1)} %reshape.115, bf16[4,2304,1024]{2,1,0:T(8,128)(2,1)} %get-tuple-element.22), kind=kOutput, calls=%fused_computation | convolution fusion | flops 150994944 | bytes 9641984 | tf_op jit(solution)/shard_map/kj,zjp->zkp/dot_general | solution.py:75
  187.4 5.2 %fusion.2 = f32[2,1024,16]{1,2,0:T(8,128)S(1)} fusion(bf16[16,2304,1]{1,0,2:T(8,128)(2,1)S(1)} %reshape.114, bf16[4,2304,1024]{2,1,0:T(8,128)(2,1)} %get-tuple-element.22), kind=kOutput, calls=%fused_computation.2 | convolution fusion | flops 150994944 | bytes 9641984 | tf_op jit(solution)/shard_map/kj,zjp->zkp/dot_general | solution.py:75
  192.6 5.8 %fusion.56 = bf16[2,1024,16]{1,2,0:T(8,128)(2,1)S(1)} fusion(f32[2,1024,16]{1,2,0:T(8,128)S(1)} %fusion, f32[2,1024,16]{1,2,0:T(8,128)S(1)} %fusion.2, bf16[16,2304,1]{1,0,2:T(8,128)(2,1)S(1)} %reshape.113, bf16[4,2304,1024]{2,1,0:T(8,128)(2,1)} %get-tuple-element.22), kind=kOutput, calls=%fused_computation.69 | convolution fusion | flops 151093248 | bytes 9838592 | tf_op jit(solution)/shard_map/kj,zjp->zkp/dot_general | solution.py:75
  199.3 1.3 fusion.8
  200.7 1.3 fusion.6
  202.0 1.3 fusion.59
  204.0 243.3 %all-reduce.4.cloned.1.call-done = f32[27,16,256]{2,0,1:T(8,128)} async-done(((f32[27,16,256]{2,0,1:T(8,128)}), f32[27,16,256]{2,0,1:T(8,128)}) %all-reduce.4.cloned.1.call-update) | async-done | bytes 442384 | tf_op jit(solution)/shard_map/psum | solution.py:78
  447.3 1.1 broadcast_multiply_fusion
  448.4 1.0 copy.48
  (60 shorter events, 8.8 us)
Async XLA Ops:
  7.2 34.9 %copy-start.6 = (bf16[27,16,256]{2,1,0:T(8,128)(2,1)S(1)}, bf16[27,16,256]{2,1,0:T(8,128)(2,1)}, u32[]{:S(2)}) copy-start(bf16[27,16,256]{2,1,0:T(8,128)(2,1)} %param.4) | copy-start | bytes 663556
  7.2 80.5 %all-gather.5.cloned.1.call-start = ((), (), s32[]{:S(2)}) async-start(), calls=%async_computation.2 | async-start | bytes 2228224 | tf_op jit(solution)/shard_map/all_gather | solution.py:68
  8.1 5.6 %collective-permute-start.2 = (bf16[1,16,1024]{2,1,0:T(8,128)(2,1)S(1)}, bf16[1,16,1024]{2,1,0:T(8,128)(2,1)S(1)}, u32[]{:S(2)}, u32[]{:S(2)}) collective-permute-start(bf16[1,16,1024]{2,1,0:T(8,128)(2,1)S(1)} %slice.138), channel_id=1, source_target_pairs={{0,16},{16,32},{32,48},{48,64},{64,80},{80,96},{96,112},{112,128},... | collective-permute-start | bytes 98312 | tf_op jit(solution)/shard_map/ppermute | solution.py:14
  11.5 5.8 %collective-permute-start.3 = (bf16[1,16,1024]{2,1,0:T(8,128)(2,1)S(1)}, bf16[1,16,1024]{2,1,0:T(8,128)(2,1)S(1)}, u32[]{:S(2)}, u32[]{:S(2)}) collective-permute-start(bf16[1,16,1024]{2,1,0:T(8,128)(2,1)S(1)} %slice.140), channel_id=1, source_target_pairs={{16,0},{32,16},{48,32},{64,48},{80,64},{96,80},{112,96},{128,112},... | collective-permute-start | bytes 98312 | tf_op jit(solution)/shard_map/ppermute | solution.py:17
  13.7 16.4 %copy-start.4 = (bf16[2,16,1024]{2,1,0:T(8,128)(2,1)}, bf16[2,16,1024]{2,1,0:T(8,128)(2,1)S(1)}, u32[]{:S(2)}) copy-start(bf16[2,16,1024]{2,1,0:T(8,128)(2,1)S(1)} %reshape.102) | copy-start | bytes 196612
  18.0 134.9 %all-gather.3.cloned.1.call-start = ((), (), s32[]{:S(2)}) async-start(), calls=%async_computation.1 | async-start | bytes 2228224 | tf_op jit(solution)/shard_map/all_gather | solution.py:50
  18.9 6.9 %collective-permute-start = (bf16[1,16,1024]{2,1,0:T(8,128)(2,1)S(1)}, bf16[1,16,1024]{2,1,0:T(8,128)(2,1)S(1)}, u32[]{:S(2)}, u32[]{:S(2)}) collective-permute-start(bf16[1,16,1024]{2,1,0:T(8,128)(2,1)S(1)} %slice.120), channel_id=1, source_target_pairs={{0,16},{16,32},{32,48},{48,64},{64,80},{80,96},{96,112},{112,128},... | collective-permute-start | bytes 98312 | tf_op jit(solution)/shard_map/ppermute | solution.py:14
  23.6 5.8 %collective-permute-start.1 = (bf16[1,16,1024]{2,1,0:T(8,128)(2,1)S(1)}, bf16[1,16,1024]{2,1,0:T(8,128)(2,1)S(1)}, u32[]{:S(2)}, u32[]{:S(2)}) collective-permute-start(bf16[1,16,1024]{2,1,0:T(8,128)(2,1)S(1)} %slice.122), channel_id=1, source_target_pairs={{16,0},{32,16},{48,32},{64,48},{80,64},{96,80},{112,96},{128,112},... | collective-permute-start | bytes 98312 | tf_op jit(solution)/shard_map/ppermute | solution.py:17
  34.6 15.0 %all-to-all-start = ((bf16[16,2,3456]{2,1,0:T(2,128)(2,1)}), bf16[16,2,3456]{2,1,0:T(2,128)(2,1)S(1)}, u32[]{:S(2)}, u32[]{:S(2)}) async-start(bf16[16,2,3456]{2,1,0:T(2,128)(2,1)} %reshape.125), calls=%async_computation | async-start | bytes 442368 | tf_op jit(solution)/shard_map/all_to_all | solution.py:46
  42.0 405.3 %all-reduce.4.cloned.1.call-start = ((), (), s32[]{:S(2)}) async-start(), calls=%async_computation.3 | async-start | bytes 1048576 | tf_op jit(solution)/shard_map/psum | solution.py:78
  87.7 3.8 copy-start.2
  157.3 2.7 copy-start.3
  170.8 1.6 copy-start.5
  172.4 6.4 %copy-start = (bf16[4,2304,1024]{2,1,0:T(8,128)(2,1)}, bf16[4,2304,1024]{2,1,0:T(8,128)(2,1)S(1)}, u32[]{:S(2)}) copy-start(bf16[4,2304,1024]{2,1,0:T(8,128)(2,1)S(1)} %fusion.27) | copy-start | bytes 56623108
  187.4 11.8 %copy-start.1 = (bf16[4,2304,1024]{2,1,0:T(8,128)(2,1)S(1)}, bf16[4,2304,1024]{2,1,0:T(8,128)(2,1)}, u32[]{:S(2)}) copy-start(bf16[4,2304,1024]{2,1,0:T(8,128)(2,1)} %copy-done) | copy-start | bytes 56623108
  192.6 6.7 %copy-start.7 = (bf16[16,2304,1]{1,0,2:T(8,128)(2,1)S(1)}, bf16[16,2304,1]{1,0,2:T(8,128)(2,1)}, u32[]{:S(2)}) copy-start(bf16[16,2304,1]{1,0,2:T(8,128)(2,1)} %reshape.111) | copy-start | bytes 221188
  199.3 1.3 copy-start.8
  200.6 1.4 copy-start.9
Sparse Core Ops, SparseCore 0:
  18.1 69.4 all-gather.4
  91.1 61.7 all-gather.2
  182.6 264.7 all-reduce.3
where the time goes:
time: 462 us; the launch traced here: 456 us
  waiting for transfers between devices  335 us (73%)
  other arithmetic  35.5 us (8%)
  matrix products  27.9 us (6%)
  local copies, waits for them, and re-layouts  25.2 us (5%)
  starting transfers between devices  18.2 us (4%)
  between operations  14.5 us (3%)
    psum x1, waiting for transfers between devices, on_device(): kernel_grad = lax.psum(kernel_acc, 'space') * scale_factor  243 us
    all_gather x1, waiting for transfers between devices, on_device(): piece = lax.all_gather(rims, 'chan', axis=1, tiled=True)  52.5 us
    unnamed x13, other arithmetic  27.2 us
    all_gather x1, waiting for transfers between devices, on_device(): piece = lax.all_gather(grad_ext, 'chan', axis=1, tiled=True)  26.7 us
    dot_general x3, matrix products, on_device(): jnp.einsum('kj,zjp->zkp', weights, window, preferred_element_type=jnp.flo...  16 us
    unnamed x26, local copies, waits for them, and re-layouts  10.9 us
  transfers between devices with their start and end apart: 8, of which 6 were waited for; matrix products, arithmetic and copies ran while one was open for 12% of the time, Pallas kernels for 0%

commit v1 on v0

v1 whole, which is shorter than its diff:
```python
import functools
import math

import jax
import jax.numpy as jnp
from jax import lax
from jax.experimental import pallas as pl
from jax.experimental.pallas import tpu as pltpu
from jax.sharding import PartitionSpec as P

MESH = pl.DeviceIdType.MESH
COPIES = 96


def col_shift(x, step, column):
    if step == 0:
        return x
    width = x.shape[1]
    if step == 1:
        moved = pltpu.roll(x, width - 1, 1)
        return jnp.where(column == 127, 0.0, moved)
    moved = pltpu.roll(x, 1, 1)
    return jnp.where(column == 0, 0.0, moved)


def row_shift(x, step):
    if step == 0:
        return x
    zeros = jnp.zeros((x.shape[0], 128), x.dtype)
    if step == 1:
        return jnp.concatenate([x[:, 128:], zeros], axis=1)
    return jnp.concatenate([zeros, x[:, :-128]], axis=1)


def tap_sum(sums_ref, sign, column):
    total = None
    for b in range(3):
        line = None
        for c in range(3):
            tap = 3 * b + c
            part = col_shift(sums_ref[16 * tap : 16 * tap + 16, :], sign * (c - 1), column)
            line = part if line is None else line + part
        moved = row_shift(line, sign * (b - 1))
        total = moved if total is None else total + moved
    return total


def layer_kernel(
    nspace,
    scale,
    vol_ref,
    cot_ref,
    ker_ref,
    kt_ref,
    out_ref,
    inp_ref,
    grad_ref,
    vg,
    cg,
    wr,
    cs,
    sums,
    part,
    near,
    quad,
    far,
    own,
    full,
    send_sem,
    recv_sem,
):
    s = lax.axis_index("space")
    c = lax.axis_index("chan")
    nz = nspace // 2
    z, x_lo = s // 2, s % 2
    x_hi, y, core = c // 8, (c // 2) % 4, c % 2
    flip = (1 - x_hi) * 8 + y * 2 + core
    mate = c + 1 - 2 * core

    def at(dz, same):
        zz = lax.rem(z + dz + nz, nz)
        xx = x_lo if same else 1 - x_lo
        return zz * 2 + xx

    pair = at(0, False)
    edge = lax.rem(s + nspace + 2 * x_lo - 1, nspace)

    def chan_of(yy):
        return x_hi * 8 + lax.rem(y + yy, 4) * 2 + core

    peers = [(s, lax.rem(c + m, 16)) for m in range(1, 16)]
    peers += [(pair, c), (pair, flip), (edge, flip)]
    for dz in (1, -1, 2, -2):
        peers += [(at(dz, True), c), (at(dz, False), c)]
    peers += [(at(4, True), c), (at(-4, True), c), (at(8, True), c)]
    barrier = pltpu.get_barrier_semaphore()
    for peer in peers:
        pl.semaphore_signal(barrier, inc=1, device_id=peer, device_id_type=MESH)

    column = lax.broadcasted_iota(jnp.int32, (16, 1024), 1) % 128
    for plane in range(2):
        local = cot_ref[plane].astype(jnp.float32)
        for tap in range(9):
            b, cc = tap // 3, tap % 3
            moved = row_shift(col_shift(local, 1 - cc, column), 1 - b)
            cs[144 * plane + 16 * tap : 144 * plane + 16 * tap + 16, :] = moved.astype(jnp.bfloat16)
    vg[1:3, x_hi, y, core] = vol_ref[...]
    cg[1:3, x_hi, y, core] = cot_ref[...]
    wr[:, c] = kt_ref[c]
    pl.semaphore_wait(barrier, len(peers))

    count = [0]
    begun = []

    def send(src, dst, peer):
        at_sem = count[0]
        count[0] += 1
        copy = pltpu.make_async_remote_copy(
            src_ref=src,
            dst_ref=dst,
            send_sem=send_sem.at[at_sem],
            recv_sem=recv_sem.at[at_sem],
            device_id=peer,
            device_id_type=MESH,
        )
        copy.start()
        begun.append(copy)
        return copy

    pair_src, pair_dst = 1 - x_lo, 3 * x_lo
    edge_src, edge_dst = x_lo, 3 * (1 - x_lo)

    v1 = [send(vol_ref, vg.at[pl.ds(1, 2), x_hi, y, core], (s, flip))]
    for to in (c, flip):
        v1.append(send(vol_ref.at[edge_src], vg.at[edge_dst, x_hi, y, core], (edge, to)))
    for to in (c, flip):
        v1.append(send(vol_ref.at[pair_src], vg.at[pair_dst, x_hi, y, core], (pair, to)))
    c1 = [
        send(cot_ref, cg.at[pl.ds(1, 2), x_hi, y, core], (s, chan_of(yy))) for yy in (1, 3, 2)
    ]

    for copy in v1:
        copy.wait_recv()
    v2 = []
    for yy in (1, 3, 2):
        v2.append(send(vg.at[:, :, y, core], vg.at[:, :, y, core], (s, chan_of(yy))))
    v3 = [send(vg.at[:, :, y, core], vg.at[:, :, y, core], (s, mate))]

    for copy in c1:
        copy.wait_recv()
    c2 = [
        send(
            cg.at[pl.ds(1, 2), x_hi, :, core],
            cg.at[pl.ds(1, 2), x_hi, :, core],
            (s, flip),
        )
    ]
    for to in (c, flip):
        c2.append(
            send(cg.at[edge_src + 1, x_hi, :, core], cg.at[edge_dst, x_hi, :, core], (edge, to))
        )
    for to in (c, flip):
        c2.append(
            send(cg.at[pair_src + 1, x_hi, :, core], cg.at[pair_dst, x_hi, :, core], (pair, to))
        )
    w1 = []
    for m in range(1, 16):
        to = lax.rem(c + m, 16)
        w1.append(send(kt_ref.at[to], wr.at[:, c], (s, to)))

    for yy, copy in zip((3, 1, 2), v2):
        copy.wait_recv()
        from_y = lax.rem(y + yy, 4)
        v3.append(send(vg.at[:, :, from_y, core], vg.at[:, :, from_y, core], (s, mate)))
    for copy in v3:
        copy.wait_recv()

    low = s == 0
    high = s == nspace - 1

    def plane_of(ref, index):
        return ref[index].reshape(256, 1024)

    def cell_dot(lhs, plane):
        return lax.dot_general(
            lhs, plane, (((1,), (1,)), ((), ())), preferred_element_type=jnp.float32
        )

    zero_rows = jnp.zeros((144, 256), jnp.float32)
    first = cell_dot(cs[0:144, :], plane_of(vg, 0))
    second = cell_dot(cs[...], plane_of(vg, 1))
    third = cell_dot(cs[...], plane_of(vg, 2))
    fourth = cell_dot(cs[144:288, :], plane_of(vg, 3))
    first = jnp.where(low, zero_rows, first)
    fourth = jnp.where(high, zero_rows, fourth)
    part[0:9] = (first + second[144:288]).reshape(9, 16, 256)
    part[9:18] = (second[0:144] + third[144:288]).reshape(9, 16, 256)
    part[18:27] = (third[0:144] + fourth).reshape(9, 16, 256)
    part[27:32] = jnp.zeros((5, 16, 256), jnp.float32)

    r = z % 4
    n1 = []
    moves = [(1, True), (-1, True), (2, True), (1, False), (-1, False), (-2, False), (0, False)]
    for slot, (dz, same) in enumerate(moves):
        group = (x_lo if same else 1 - x_lo) * 4 + (r + dz + 4) % 4
        n1.append(send(part.at[pl.ds(group * 4, 4)], near.at[slot], (at(dz, same), c)))

    def conv(weights, ref, first_plane):
        rows = ref[first_plane : first_plane + 3].reshape(768, 1024)
        sums[...] = jnp.dot(weights, rows, preferred_element_type=jnp.float32)

    blank = jnp.zeros((144, 256), jnp.bfloat16)

    def edge_weights(taps, plane):
        below, middle, above = taps
        if plane == 0:
            below = jnp.where(low, blank, below)
        else:
            above = jnp.where(high, blank, above)
        return jnp.concatenate([below, middle, above], axis=1)

    forward = [ker_ref[9 * a : 9 * a + 9].reshape(144, 256) for a in range(3)]
    for plane in range(2):
        conv(edge_weights(forward, plane), vg, plane)
        out_ref[plane] = tap_sum(sums, 1, column).astype(jnp.bfloat16)

    for copy in c2:
        copy.wait_recv()
    c3 = send(cg.at[:, :, :, core], cg.at[:, :, :, core], (s, mate))

    for copy in n1:
        copy.wait_recv()
    zi = z // 4
    mine = x_lo * 4 + r
    total = part[pl.ds(mine * 4, 4)]
    for slot in range(7):
        total = total + near[slot]
    quad[...] = total
    f1 = []
    for slot, step in enumerate((1, 3, 2)):
        f1.append(
            send(quad.at[(zi + step) % 4], far.at[slot], (at((4, -4, 8)[slot], True), c))
        )
    for copy in f1:
        copy.wait_recv()
    mean = (quad[zi] + far[0] + far[1] + far[2]) * scale
    own[zi] = mean
    a1 = []
    for dz in (4, -4, 8):
        a1.append(send(own.at[zi], own.at[zi], (at(dz, True), c)))

    c3.wait_recv()
    for copy in w1:
        copy.wait_recv()
    backward = [wr[2 - a].reshape(256, 144).T for a in range(3)]
    for plane in range(2):
        conv(edge_weights(backward, plane), cg, plane)
        inp_ref[plane] = tap_sum(sums, -1, column).astype(jnp.bfloat16)

    for copy in a1:
        copy.wait_recv()
    full[pl.ds(mine * 4, 4)] = own[...]
    a2 = []
    for dz, same in moves:
        a2.append(send(own, full.at[pl.ds(mine * 4, 4)], (at(dz, same), c)))
    for copy in a2:
        copy.wait_recv()
    grad_ref[...] = full[0:27]
    for copy in begun:
        copy.wait_send()


def on_device(volume, kernel, cotangent):
    depth, chans, height, width = volume.shape
    cells = height * width
    nspace = lax.axis_size("space")
    scale = 1.0 / math.sqrt(depth * nspace * cells)
    vol = volume.reshape(depth, chans, cells)
    cot = cotangent.reshape(depth, chans, cells)
    kt = kernel.reshape(3, 9, 16, 16, 16).transpose(3, 0, 2, 1, 4).reshape(16, 3, 16, 144)
    vmem = pl.BlockSpec(memory_space=pltpu.VMEM)
    bf16, f32 = jnp.bfloat16, jnp.float32
    out, inp, grad = pl.pallas_call(
        functools.partial(layer_kernel, nspace, scale),
        out_shape=(
            jax.ShapeDtypeStruct((2, 16, 1024), bf16),
            jax.ShapeDtypeStruct((2, 16, 1024), bf16),
            jax.ShapeDtypeStruct((27, 16, 256), f32),
        ),
        in_specs=[vmem] * 4,
        out_specs=(vmem,) * 3,
        scratch_shapes=[
            pltpu.VMEM((4, 2, 4, 2, 16, 1024), bf16),
            pltpu.VMEM((4, 2, 4, 2, 16, 1024), bf16),
            pltpu.VMEM((3, 16, 16, 144), bf16),
            pltpu.VMEM((288, 1024), bf16),
            pltpu.VMEM((144, 1024), f32),
            pltpu.VMEM((32, 16, 256), f32),
            pltpu.VMEM((7, 4, 16, 256), f32),
            pltpu.VMEM((4, 16, 256), f32),
            pltpu.VMEM((3, 16, 256), f32),
            pltpu.VMEM((4, 16, 256), f32),
            pltpu.VMEM((32, 16, 256), f32),
            pltpu.SemaphoreType.DMA((COPIES,)),
            pltpu.SemaphoreType.DMA((COPIES,)),
        ],
        compiler_params=pltpu.CompilerParams(
            collective_id=0, has_side_effects=True, vmem_limit_bytes=48 << 20
        ),
        name="layer",
    )(vol, cot, kernel, kt)
    return (
        out.reshape(depth, chans, height, width),
        inp.reshape(depth, chans, height, width),
        grad,
    )


def solution(mesh):
    return jax.shard_map(
        on_device,
        mesh=mesh,
        in_specs=(
            P("space", "chan", None, None),
            P(None, "chan", None),
            P("space", "chan", None, None),
        ),
        out_specs=(
            P("space", "chan", None, None),
            P("space", "chan", None, None),
            P(None, "chan", None),
        ),
        check_vma=False,
    )
```

time: 462 us -> 82.9 us (0.18)
  the two profiles are of different devices: /device:TPU:8 before, /device:TPU:1 now
where the time goes in v1:
time: 82.9 us; the launch traced here: 81.4 us
  Pallas kernels  71.1 us (86%)
  local copies, waits for them, and re-layouts  9.59 us (12%)
    pallas_call x1, Pallas kernels, on_device(): pl.pallas_call(functools.partial(layer_kernel, nspace, scale), out_shape=...  71.1 us
    reshape x3, local copies, waits for them, and re-layouts, on_device(): kernel.reshape(3, 9, 16, 16, 16).transpose(3, 0, 2, 1, 4)  7.46 us
    unnamed x9, local copies, waits for them, and re-layouts  2.06 us

profile of v1, /device:TPU:1, one launch (start us, length us, event | category | flops | bytes accessed | tf_op | source)
XLA Modules:
  0.0 81.4 jit_solution(14674675514930351924)
XLA Ops:
  0.6 3.2 %reshape.26 = bf16[3,9,16,16,16]{4,3,2,1,0:T(8,128)(2,1)} reshape(bf16[27,16,256]{2,1,0:T(8,128)(2,1)} %ker_ref.1) | data formatting | bytes 442368 | tf_op jit(solution)/shard_map/reshape | solution.py:280
  3.8 3.3 %copy.7 = bf16[3,9,16,16,16]{2,4,1,0,3:T(8,128)(2,1)S(1)} copy(bf16[3,9,16,16,16]{4,3,2,1,0:T(8,128)(2,1)} %reshape.26) | data formatting | bytes 442368 | tf_op jit(solution)/shard_map/reshape | solution.py:280
  7.1 0.0 copy-start.1
  7.1 0.0 copy-start.2
  7.1 0.0 copy-start
  7.1 1.0 %copy.8.kt_ref = bf16[16,3,16,144]{3,2,1,0:T(8,128)(2,1)S(1)} copy(bf16[16,3,16,144]{2,3,1,0:T(8,128)(2,1)S(1)} %bitcast.17) | data formatting | bytes 442368 | tf_op jit(solution)/shard_map/reshape | solution.py:280
  8.1 0.0 copy-done.1
  8.2 0.0 copy-done.2
  8.2 0.0 copy-done
  8.3 71.1 %layer.1 = (bf16[2,16,1024]{2,1,0:T(8,128)(2,1)S(1)}, bf16[2,16,1024]{2,1,0:T(8,128)(2,1)S(1)}, f32[27,16,256]{2,1,0:T(8,128)S(1)}) custom-call(bf16[2,16,1024]{2,1,0:T(8,128)(2,1)S(1)} %reshape.24.vol_ref, bf16[2,16,1024]{2,1,0:T(8,128)(2,1)S(1)} %reshape.25.cot_ref, bf16[27,16,256]{2,1,0:T(8,128)(2,1)S(1)} %copy-done, bf16[16,3,16,144]{3,2,1,0:T(8,128)(2,1)S(1)} %copy.8.kt_ref), custom_call_target="tpu_custom_call" | custom-call | tf_op jit(solution)/shard_map/layer/pallas_call | solution.py:283
  79.4 0.6 copy.10
  80.0 0.6 copy.9
  80.7 0.8 copy.12
  (2 shorter events, 0.1 us)
Async XLA Ops:
  7.1 1.1 %copy-start.1 = (bf16[2,16,8,128]{3,2,1,0:T(8,128)(2,1)S(1)}, bf16[2,16,8,128]{3,2,1,0:T(8,128)(2,1)}, u32[]{:S(2)}) copy-start(bf16[2,16,8,128]{3,2,1,0:T(8,128)(2,1)} %param.3) | copy-start | bytes 196612
  7.1 1.1 %copy-start.2 = (bf16[2,16,8,128]{3,2,1,0:T(8,128)(2,1)S(1)}, bf16[2,16,8,128]{3,2,1,0:T(8,128)(2,1)}, u32[]{:S(2)}) copy-start(bf16[2,16,8,128]{3,2,1,0:T(8,128)(2,1)} %param.5) | copy-start | bytes 196612
  7.1 1.1 %copy-start = (bf16[27,16,256]{2,1,0:T(8,128)(2,1)S(1)}, bf16[27,16,256]{2,1,0:T(8,128)(2,1)}, u32[]{:S(2)}) copy-start(bf16[27,16,256]{2,1,0:T(8,128)(2,1)} %ker_ref.1) | copy-start | bytes 663556

commit v2 on v1

v2 whole, which is shorter than its diff:
```python
import functools
import math

import jax
import jax.numpy as jnp
from jax import lax
from jax.experimental import pallas as pl
from jax.experimental.pallas import tpu as pltpu
from jax.sharding import PartitionSpec as P

MESH = pl.DeviceIdType.MESH
COPIES = 96


def col_shift(x, step, column):
    if step == 0:
        return x
    width = x.shape[1]
    if step == 1:
        moved = pltpu.roll(x, width - 1, 1)
        return jnp.where(column == 127, 0.0, moved)
    moved = pltpu.roll(x, 1, 1)
    return jnp.where(column == 0, 0.0, moved)


def row_shift(x, step):
    if step == 0:
        return x
    zeros = jnp.zeros((x.shape[0], 128), x.dtype)
    if step == 1:
        return jnp.concatenate([x[:, 128:], zeros], axis=1)
    return jnp.concatenate([zeros, x[:, :-128]], axis=1)


def tap_sum(sums_ref, sign, column):
    total = None
    for b in range(3):
        line = None
        for c in range(3):
            tap = 3 * b + c
            part = col_shift(sums_ref[16 * tap : 16 * tap + 16, :], sign * (c - 1), column)
            line = part if line is None else line + part
        moved = row_shift(line, sign * (b - 1))
        total = moved if total is None else total + moved
    return total


def layer_kernel(
    nspace,
    scale,
    vol_ref,
    cot_ref,
    ker_ref,
    out_ref,
    inp_ref,
    grad_ref,
    vg,
    cg,
    kt,
    wr,
    cs,
    sums,
    part,
    near,
    quad,
    far,
    own,
    full,
    send_sem,
    recv_sem,
    known_sem,
):
    s = lax.axis_index("space")
    c = lax.axis_index("chan")
    nz = nspace // 2
    z, x_lo = s // 2, s % 2
    x_hi, y, core = c // 8, (c // 2) % 4, c % 2
    flip = (1 - x_hi) * 8 + y * 2 + core
    mate = c + 1 - 2 * core

    def at(dz, same):
        zz = lax.rem(z + dz + nz, nz)
        xx = x_lo if same else 1 - x_lo
        return zz * 2 + xx

    pair = at(0, False)
    edge = lax.rem(s + nspace + 2 * x_lo - 1, nspace)

    def y_at(dy):
        return lax.rem(y + dy, 4)

    def chan_of(dy):
        return x_hi * 8 + y_at(dy) * 2 + core

    peers = [(s, mate), (s, flip)] + [(s, chan_of(dy)) for dy in (1, 2, 3)]
    peers += [(pair, c), (pair, flip), (edge, c), (edge, flip)]
    peers += [(at(1, True), c), (at(-1, True), c)]
    barrier = pltpu.get_barrier_semaphore()
    for peer in peers:
        pl.semaphore_signal(barrier, inc=1, device_id=peer, device_id_type=MESH)

    column = lax.broadcasted_iota(jnp.int32, (16, 1024), 1) % 128
    for plane in range(2):
        local = cot_ref[plane].astype(jnp.float32)
        for tap in range(9):
            b, cc = tap // 3, tap % 3
            moved = row_shift(col_shift(local, 1 - cc, column), 1 - b)
            cs[144 * plane + 16 * tap : 144 * plane + 16 * tap + 16, :] = moved.astype(jnp.bfloat16)
    vg[1:3, x_hi, y, core] = vol_ref[...]
    cg[1:3, x_hi, y, core] = cot_ref[...]
    taps = [ker_ref[t].astype(jnp.float32) for t in range(27)]
    filler = jnp.zeros((16, 80), jnp.float32)
    for to in range(16):
        lanes = slice(16 * to, 16 * to + 16)
        for a in range(3):
            row = jnp.concatenate([taps[9 * a + t][:, lanes] for t in range(8)], axis=1)
            kt[to, a] = row.astype(jnp.bfloat16)
        row = jnp.concatenate([taps[9 * a + 8][:, lanes] for a in range(3)] + [filler], axis=1)
        kt[to, 3] = row.astype(jnp.bfloat16)
    wr[:, c] = kt[c]
    pl.semaphore_wait(barrier, len(peers))

    def tell(stage, dz):
        for step in (dz, -dz):
            pl.semaphore_signal(
                known_sem.at[stage], inc=1, device_id=(at(step, True), c), device_id_type=MESH
            )

    tell(0, 1)

    count = [0]
    sent = []

    def copy_of(src, dst, peer, index=None):
        if index is None:
            index = count[0]
            count[0] += 1
        return pltpu.make_async_remote_copy(
            src_ref=src,
            dst_ref=dst,
            send_sem=send_sem.at[index],
            recv_sem=recv_sem.at[index],
            device_id=peer,
            device_id_type=MESH,
        )

    def send(src, dst, peer):
        copy = copy_of(src, dst, peer)
        copy.start()
        sent.append(copy)
        return copy

    def start(copies):
        for copy in copies:
            copy.start()

    def arrive(copies):
        for copy in copies:
            copy.wait_recv()

    def by_core(on_0, on_1):
        pl.when(core == 0)(on_0)
        pl.when(core == 1)(on_1)

    pair_src, pair_dst = 1 - x_lo, 3 * x_lo
    edge_src, edge_dst = x_lo, 3 * (1 - x_lo)
    middle = pl.ds(1, 2)

    def x_first(ref, g, lane):
        one = [copy_of(ref, g.at[middle, x_hi, y, lane], (s, flip))]
        for to in (c, flip):
            one.append(copy_of(ref.at[edge_src], g.at[edge_dst, x_hi, y, lane], (edge, to)))
        for to in (c, flip):
            one.append(copy_of(ref.at[pair_src], g.at[pair_dst, x_hi, y, lane], (pair, to)))
        block = g.at[:, :, y, lane]
        two = [copy_of(block, block, (s, chan_of(dy))) for dy in (1, 3, 2)]
        return one, two

    def y_first(ref, g, lane):
        one = [copy_of(ref, g.at[middle, x_hi, y, lane], (s, chan_of(dy))) for dy in (1, 3, 2)]
        block = g.at[middle, x_hi, :, lane]
        two = [copy_of(block, block, (s, flip))]
        for to in (c, flip):
            src = g.at[edge_src + 1, x_hi, :, lane]
            two.append(copy_of(src, g.at[edge_dst, x_hi, :, lane], (edge, to)))
        for to in (c, flip):
            src = g.at[pair_src + 1, x_hi, :, lane]
            two.append(copy_of(src, g.at[pair_dst, x_hi, :, lane], (pair, to)))
        return one, two

    def hand(blocks, lane_sems=None):
        return [
            copy_of(block, block, (s, mate), None if lane_sems is None else lane_sems[i])
            for i, block in enumerate(blocks)
        ]

    v0_one, v0_two = x_first(vol_ref, vg, 0)
    v1_one, v1_two = y_first(vol_ref, vg, 1)
    sems = list(range(count[0], count[0] + 4))
    count[0] += 4
    v0_hand = hand([vg.at[:, :, y_at(dy), 0] for dy in (0, 3, 1, 2)], sems)
    v1_hand = hand(
        [
            vg.at[middle, x_hi, :, 1],
            vg.at[middle, 1 - x_hi, :, 1],
            vg.at[3 * x_lo, :, :, 1],
            vg.at[3 * (1 - x_lo), :, :, 1],
        ],
        sems,
    )
    by_core(lambda: start(v0_one), lambda: start(v1_one))

    def v0_middle():
        arrive(v0_one)
        start(v0_two)
        v0_hand[0].start()

    def v1_middle():
        arrive(v1_one)
        start(v1_two)
        v1_hand[0].start()

    by_core(v0_middle, v1_middle)
    pl.semaphore_wait(known_sem.at[0], 2)
    tell(1, 2)

    def v0_late():
        for i in range(3):
            v0_two[i].wait_recv()
            v0_hand[i + 1].start()

    def v1_late():
        v1_two[0].wait_recv()
        v1_hand[1].start()
        arrive(v1_two[1:3])
        v1_hand[2].start()
        arrive(v1_two[3:5])
        v1_hand[3].start()

    by_core(v0_late, v1_late)

    c_one, c_two = x_first(cot_ref, cg, core)
    c_hand = hand([cg.at[:, :, y_at(dy), core] for dy in (0, 3, 1, 2)])
    start(c_one)
    pl.semaphore_wait(known_sem.at[1], 2)
    tell(2, 4)
    arrive(v0_hand)

    low = s == 0
    high = s == nspace - 1

    def plane_of(ref, index):
        return ref[index].reshape(256, 1024)

    def cell_dot(lhs, plane):
        return lax.dot_general(
            lhs, plane, (((1,), (1,)), ((), ())), preferred_element_type=jnp.float32
        )

    zero_rows = jnp.zeros((144, 256), jnp.float32)
    first = cell_dot(cs[0:144, :], plane_of(vg, 0))
    second = cell_dot(cs[...], plane_of(vg, 1))
    third = cell_dot(cs[...], plane_of(vg, 2))
    fourth = cell_dot(cs[144:288, :], plane_of(vg, 3))
    first = jnp.where(low, zero_rows, first)
    fourth = jnp.where(high, zero_rows, fourth)
    terms = [first + second[144:288], second[0:144] + third[144:288], third[0:144] + fourth]
    for a in range(3):
        term = terms[a].reshape(9, 2, 8, 256)
        for half in range(2):
            part[half, 9 * a : 9 * a + 9] = term[:, half]
    part[:, 27:32] = jnp.zeros((2, 5, 8, 256), jnp.float32)

    r = z % 4
    zi = z // 4
    mine = pl.ds((x_lo * 4 + r) * 4, 4)
    moves = [(1, True), (-1, True), (2, True), (1, False), (-1, False), (-2, False), (0, False)]
    n1 = []
    for half in range(2):
        n1.append([])
        for slot, (dz, same) in enumerate(moves):
            group = (x_lo if same else 1 - x_lo) * 4 + (r + dz + 4) % 4
            n1[half].append(
                send(part.at[half, pl.ds(group * 4, 4)], near.at[half, slot], (at(dz, same), c))
            )

    arrive(c_one)
    start(c_two)
    c_hand[0].start()

    def conv(weights, ref, first_plane):
        rows = ref[first_plane : first_plane + 3].reshape(768, 1024)
        sums[...] = jnp.dot(weights, rows, preferred_element_type=jnp.float32)

    blank = jnp.zeros((144, 256), jnp.bfloat16)

    def edge_weights(taps, plane):
        below, middle, above = taps
        if plane == 0:
            below = jnp.where(low, blank, below)
        else:
            above = jnp.where(high, blank, above)
        return jnp.concatenate([below, middle, above], axis=1)

    forward = [ker_ref[9 * a : 9 * a + 9].reshape(144, 256) for a in range(3)]
    for plane in range(2):
        conv(edge_weights(forward, plane), vg, plane)
        out_ref[plane] = tap_sum(sums, 1, column).astype(jnp.bfloat16)

    pl.semaphore_wait(known_sem.at[2], 2)
    f1 = []
    for half in range(2):
        arrive(n1[half])
        total = part[half, mine]
        for slot in range(7):
            total = total + near[half, slot]
        quad[half] = total
        f1.append(
            [
                send(quad.at[half, (zi + step) % 4], far.at[half, slot], (at(dz, True), c))
                for slot, (step, dz) in enumerate(((1, 4), (3, -4), (2, 8)))
            ]
        )

    w1 = []
    for m in range(1, 16):
        to = lax.rem(c + m, 16)
        w1.append(send(kt.at[to], wr.at[:, c], (s, to)))

    a1 = []
    for half in range(2):
        arrive(f1[half])
        total = quad[half, zi] + far[half, 0] + far[half, 1] + far[half, 2]
        own[half, zi] = total * scale
        a1.append(
            [send(own.at[half, zi], own.at[half, zi], (at(dz, True), c)) for dz in (4, -4, 8)]
        )

    for i in range(3):
        c_two[i].wait_recv()
        c_hand[i + 1].start()

    a2 = []
    for half in range(2):
        arrive(a1[half])
        full[half, mine] = own[half]
        for dz, same in moves:
            a2.append(send(own.at[half], full.at[half, mine], (at(dz, same), c)))

    arrive(c_hand)
    arrive(w1)
    last = wr[3].reshape(256, 128)
    backward = []
    for a in (2, 1, 0):
        lines = jnp.concatenate(
            [wr[a].reshape(256, 128), last[:, 16 * a : 16 * a + 16]], axis=1
        )
        backward.append(lines.T)
    for plane in range(2):
        conv(edge_weights(backward, plane), cg, plane)
        inp_ref[plane] = tap_sum(sums, -1, column).astype(jnp.bfloat16)

    arrive(a2)
    for half in range(2):
        grad_ref[:, 8 * half : 8 * half + 8] = full[half, 0:27]

    def ended(copies):
        for copy in copies:
            copy.wait_send()

    by_core(
        lambda: ended(v0_one + v0_two + v0_hand),
        lambda: ended(v1_one + v1_two + v1_hand),
    )
    ended(c_one + c_two + c_hand + sent)


def on_device(volume, kernel, cotangent):
    depth, chans, height, width = volume.shape
    cells = height * width
    nspace = lax.axis_size("space")
    scale = 1.0 / math.sqrt(depth * nspace * cells)
    vol = volume.reshape(depth, chans, cells)
    cot = cotangent.reshape(depth, chans, cells)
    vmem = pl.BlockSpec(memory_space=pltpu.VMEM)
    bf16, f32 = jnp.bfloat16, jnp.float32
    out, inp, grad = pl.pallas_call(
        functools.partial(layer_kernel, nspace, scale),
        out_shape=(
            jax.ShapeDtypeStruct((2, 16, 1024), bf16),
            jax.ShapeDtypeStruct((2, 16, 1024), bf16),
            jax.ShapeDtypeStruct((27, 16, 256), f32),
        ),
        in_specs=[vmem] * 3,
        out_specs=(vmem,) * 3,
        scratch_shapes=[
            pltpu.VMEM((4, 2, 4, 2, 16, 1024), bf16),
            pltpu.VMEM((4, 2, 4, 2, 16, 1024), bf16),
            pltpu.VMEM((16, 4, 16, 128), bf16),
            pltpu.VMEM((4, 16, 16, 128), bf16),
            pltpu.VMEM((288, 1024), bf16),
            pltpu.VMEM((144, 1024), f32),
            pltpu.VMEM((2, 32, 8, 256), f32),
            pltpu.VMEM((2, 7, 4, 8, 256), f32),
            pltpu.VMEM((2, 4, 8, 256), f32),
            pltpu.VMEM((2, 3, 8, 256), f32),
            pltpu.VMEM((2, 4, 8, 256), f32),
            pltpu.VMEM((2, 32, 8, 256), f32),
            pltpu.SemaphoreType.DMA((COPIES,)),
            pltpu.SemaphoreType.DMA((COPIES,)),
            pltpu.SemaphoreType.REGULAR((3,)),
        ],
        compiler_params=pltpu.CompilerParams(
            collective_id=0, has_side_effects=True, vmem_limit_bytes=48 << 20
        ),
        name="layer",
    )(vol, cot, kernel)
    return (
        out.reshape(depth, chans, height, width),
        inp.reshape(depth, chans, height, width),
        grad,
    )


def solution(mesh):
    return jax.shard_map(
        on_device,
        mesh=mesh,
        in_specs=(
            P("space", "chan", None, None),
            P(None, "chan", None),
            P("space", "chan", None, None),
        ),
        out_specs=(
            P("space", "chan", None, None),
            P("space", "chan", None, None),
            P(None, "chan", None),
        ),
        check_vma=False,
    )
```

time: 82.9 us -> 63.4 us (0.76)
  Pallas kernels: 71.1 us -> 58.2 us
  local copies, waits for them, and re-layouts: 9.59 us -> 3.83 us
    pallas_call x1, Pallas kernels: 71.1 us -> 58.2 us  [on_device(): pl.pallas_call(functools.partial(layer_kernel, nspace, scale), out_shape=...]
    reshape x3 -> x0, local copies, waits for them, and re-layouts: 7.46 us -> none  [on_device(): kernel.reshape(3, 9, 16, 16, 16).transpose(3, 0, 2, 1, 4)]
    reshape x1, local copies, waits for them, and re-layouts: 0.03 us -> 0.91 us  [on_device(): vol = volume.reshape(depth, chans, cells)]
    reshape x1, local copies, waits for them, and re-layouts: 0.03 us -> 0.87 us  [on_device(): cot = cotangent.reshape(depth, chans, cells)]
    unnamed x9 -> x5, local copies, waits for them, and re-layouts: 2.06 us -> 2.05 us
where the time goes in v2:
time: 63.4 us; the launch traced here: 62.7 us
  Pallas kernels  58.2 us (92%)
  local copies, waits for them, and re-layouts  3.83 us (6%)
  between operations  0.66 us (1%)
    pallas_call x1, Pallas kernels, on_device(): pl.pallas_call(functools.partial(layer_kernel, nspace, scale), out_shape=...  58.2 us
    unnamed x5, local copies, waits for them, and re-layouts  2.05 us

profile of v2, /device:TPU:1, one launch (start us, length us, event | category | flops | bytes accessed | tf_op | source)
XLA Modules:
  0.0 62.7 jit_solution(465904632344487533)
XLA Ops:
  0.6 0.0 copy-start
  0.6 0.9 %reshape.18.vol_ref = bf16[2,16,1024]{2,1,0:T(8,128)(2,1)S(1)} reshape(bf16[2,16,8,128]{3,2,1,0:T(8,128)(2,1)} %param.3) | data formatting | bytes 131072 | tf_op jit(solution)/shard_map/reshape | solution.py:383
  1.6 0.9 %reshape.19.cot_ref = bf16[2,16,1024]{2,1,0:T(8,128)(2,1)S(1)} reshape(bf16[2,16,8,128]{3,2,1,0:T(8,128)(2,1)} %param.5) | data formatting | bytes 131072 | tf_op jit(solution)/shard_map/reshape | solution.py:384
  2.4 0.0 copy-done
  2.4 58.2 %layer.1 = (bf16[2,16,1024]{2,1,0:T(8,128)(2,1)S(1)}, bf16[2,16,1024]{2,1,0:T(8,128)(2,1)S(1)}, f32[27,16,256]{2,1,0:T(8,128)S(1)}) custom-call(bf16[2,16,1024]{2,1,0:T(8,128)(2,1)S(1)} %reshape.18.vol_ref, bf16[2,16,1024]{2,1,0:T(8,128)(2,1)S(1)} %reshape.19.cot_ref, bf16[27,16,256]{2,1,0:T(8,128)(2,1)S(1)} %copy-done), custom_call_target="tpu_custom_call" | custom-call | tf_op jit(solution)/shard_map/layer/pallas_call | solution.py:387
  60.7 0.6 %copy.6 = bf16[4,8,8,128]{3,2,1,0:T(8,128)(2,1)} copy(bf16[4,8,8,128]{3,1,2,0:T(8,128)(2,1)S(1)} %bitcast.13) | data formatting | bytes 131072
  61.3 0.6 %copy.7 = bf16[4,8,8,128]{3,2,1,0:T(8,128)(2,1)} copy(bf16[4,8,8,128]{3,1,2,0:T(8,128)(2,1)S(1)} %bitcast.12) | data formatting | bytes 131072
  62.0 0.8 %copy.9 = f32[27,16,256]{2,1,0:T(8,128)} copy(f32[27,16,256]{2,1,0:T(8,128)S(1)} %get-tuple-element.14) | data formatting | bytes 884736
Async XLA Ops:
  0.6 1.8 %copy-start = (bf16[27,16,256]{2,1,0:T(8,128)(2,1)S(1)}, bf16[27,16,256]{2,1,0:T(8,128)(2,1)}, u32[]{:S(2)}) copy-start(bf16[27,16,256]{2,1,0:T(8,128)(2,1)} %ker_ref.1) | copy-start | bytes 663556

commit v3 on v2

v3 whole, which is shorter than its diff:
```python
import functools
import math

import jax
import jax.numpy as jnp
from jax import lax
from jax.experimental import pallas as pl
from jax.experimental.pallas import tpu as pltpu
from jax.sharding import PartitionSpec as P

MESH = pl.DeviceIdType.MESH
COPIES = 112


def col_shift(x, step, column):
    if step == 0:
        return x
    width = x.shape[1]
    if step == 1:
        moved = pltpu.roll(x, width - 1, 1)
        return jnp.where(column == 127, 0.0, moved)
    moved = pltpu.roll(x, 1, 1)
    return jnp.where(column == 0, 0.0, moved)


def row_shift(x, step):
    if step == 0:
        return x
    zeros = jnp.zeros((x.shape[0], 128), x.dtype)
    if step == 1:
        return jnp.concatenate([x[:, 128:], zeros], axis=1)
    return jnp.concatenate([zeros, x[:, :-128]], axis=1)


def tap_sum(sums_ref, sign, column):
    total = None
    for b in range(3):
        line = None
        for c in range(3):
            tap = 3 * b + c
            part = col_shift(sums_ref[16 * tap : 16 * tap + 16, :], sign * (c - 1), column)
            line = part if line is None else line + part
        moved = row_shift(line, sign * (b - 1))
        total = moved if total is None else total + moved
    return total


def layer_kernel(
    nspace,
    scale,
    vol_ref,
    cot_ref,
    ker_ref,
    out_ref,
    inp_ref,
    grad_ref,
    vol,
    cot,
    rim,
    vg,
    cg,
    kt,
    wr,
    cs,
    sums,
    part,
    near,
    quad,
    far,
    own,
    full,
    send_sem,
    recv_sem,
    known_sem,
):
    s = lax.axis_index("space")
    c = lax.axis_index("chan")
    nz = nspace // 2
    z, x_lo = s // 2, s % 2
    x_hi, y, core = c // 8, (c // 2) % 4, c % 2
    flip = (1 - x_hi) * 8 + y * 2 + core
    mate = c + 1 - 2 * core

    def at(dz, same):
        zz = lax.rem(z + dz + nz, nz)
        xx = x_lo if same else 1 - x_lo
        return zz * 2 + xx

    pair = at(0, False)
    edge = lax.rem(s + nspace + 2 * x_lo - 1, nspace)

    def y_at(dy):
        return lax.rem(y + dy, 4)

    def chan_of(dy):
        return x_hi * 8 + y_at(dy) * 2 + core

    peers = [(s, mate), (s, flip)] + [(s, chan_of(dy)) for dy in (1, 2, 3)]
    peers += [(pair, c), (pair, flip), (edge, c), (edge, flip)]
    peers += [(at(1, True), c), (at(-1, True), c)]
    barrier = pltpu.get_barrier_semaphore()
    for peer in peers:
        pl.semaphore_signal(barrier, inc=1, device_id=peer, device_id_type=MESH)

    for plane in range(2):
        block = vol_ref[plane].astype(jnp.float32).reshape(16, 1024)
        vol[plane] = block.astype(jnp.bfloat16)
        vg[plane, x_hi, y, core] = block.astype(jnp.bfloat16)
        block = cot_ref[plane].astype(jnp.float32).reshape(16, 1024)
        cot[plane] = block.astype(jnp.bfloat16)
        cg[plane, x_hi, y, core] = block.astype(jnp.bfloat16)
    pl.semaphore_wait(barrier, len(peers))

    count = [0]
    sent = []

    def copy_of(src, dst, peer, index=None):
        if index is None:
            index = count[0]
            count[0] += 1
        return pltpu.make_async_remote_copy(
            src_ref=src,
            dst_ref=dst,
            send_sem=send_sem.at[index],
            recv_sem=recv_sem.at[index],
            device_id=peer,
            device_id_type=MESH,
        )

    def send(src, dst, peer):
        copy = copy_of(src, dst, peer)
        copy.start()
        sent.append(copy)
        return copy

    def start(copies):
        for copy in copies:
            copy.start()

    def arrive(copies):
        for copy in copies:
            copy.wait_recv()

    def ended(copies):
        for copy in copies:
            copy.wait_send()

    def by_core(on_0, on_1):
        pl.when(core == 0)(on_0)
        pl.when(core == 1)(on_1)

    def tell(stage, dz):
        for step in (dz, -dz):
            pl.semaphore_signal(
                known_sem.at[stage], inc=1, device_id=(at(step, True), c), device_id_type=MESH
            )

    pair_src, pair_dst = 1 - x_lo, 2 + x_lo
    edge_src, edge_dst = x_lo, 3 - x_lo
    mine, rims = pl.ds(0, 2), pl.ds(2, 2)

    def hand(blocks, shared=None):
        return [
            copy_of(block, block, (s, mate), None if shared is None else shared[i])
            for i, block in enumerate(blocks)
        ]

    def to_y(src, dst):
        return [copy_of(src, dst, (s, chan_of(dy))) for dy in (1, 3, 2)]

    def to_rims(sources, targets):
        copies = [copy_of(sources[0], targets[0], (edge, to)) for to in (c, flip)]
        return copies + [copy_of(sources[1], targets[1], (pair, to)) for to in (c, flip)]

    def own_rims(block, g, lane):
        return to_rims(
            (block.at[edge_src], block.at[pair_src]),
            (g.at[edge_dst, x_hi, y, lane], g.at[pair_dst, x_hi, y, lane]),
        )

    def shared_sems():
        count[0] += 4
        return list(range(count[0] - 4, count[0]))

    v0_one = [copy_of(vol, vg.at[mine, x_hi, y, 0], (s, flip))]
    v0_two = to_y(vg.at[mine, :, y, 0], vg.at[mine, :, y, 0])
    v1_one = to_y(vol, vg.at[mine, x_hi, y, 1])
    v1_two = [
        copy_of(vg.at[p, x_hi, :, 1], vg.at[p, x_hi, :, 1], (s, flip)) for p in range(2)
    ]
    sems = shared_sems()
    v0_hand = hand([vg.at[mine, :, y_at(dy), 0] for dy in (0, 3, 1, 2)], sems)
    v1_hand = hand(
        [vg.at[p, side, :, 1] for side in (x_hi, 1 - x_hi) for p in range(2)], sems
    )
    by_core(lambda: start(v0_one), lambda: start(v1_one))
    beside = [
        send(cot.at[edge_src], rim.at[edge_dst - 2], (edge, c)),
        send(cot.at[pair_src], rim.at[pair_dst - 2], (pair, c)),
    ]
    tell(0, 1)

    column = lax.broadcasted_iota(jnp.int32, (16, 1024), 1) % 128
    low = s == 0
    high = s == nspace - 1

    def spread(block, slot):
        for tap in range(9):
            b, cc = tap // 3, tap % 3
            moved = row_shift(col_shift(block, 1 - cc, column), 1 - b)
            first = 144 * slot + 16 * tap
            cs[first : first + 16, :] = moved.astype(jnp.bfloat16)

    for plane in range(2):
        spread(cot[plane].astype(jnp.float32), plane + 1)

    def v0_middle():
        arrive(v0_one)
        start(v0_two)
        v0_hand[0].start()

    def v1_middle():
        arrive(v1_one)
        start(v1_two)
        start(v1_hand[0:2])

    by_core(v0_middle, v1_middle)

    taps = [ker_ref[t].astype(jnp.float32) for t in range(27)]
    filler = jnp.zeros((16, 80), jnp.float32)
    for to in range(16):
        lanes = slice(16 * to, 16 * to + 16)
        for a in range(3):
            row = jnp.concatenate([taps[9 * a + t][:, lanes] for t in range(8)], axis=1)
            kt[to, a] = row.astype(jnp.bfloat16)
        row = jnp.concatenate([taps[9 * a + 8][:, lanes] for a in range(3)] + [filler], axis=1)
        kt[to, 3] = row.astype(jnp.bfloat16)
    wr[:, c] = kt[c]

    pl.semaphore_wait(known_sem.at[0], 2)
    tell(1, 2)
    arrive(beside)
    below = rim[0].astype(jnp.float32)
    above = rim[1].astype(jnp.float32)
    spread(jnp.where(low, jnp.zeros_like(below), below), 0)
    spread(jnp.where(high, jnp.zeros_like(above), above), 3)

    def v0_late():
        for i in range(3):
            v0_two[i].wait_recv()
            v0_hand[i + 1].start()

    def v1_late():
        for i in range(2):
            v1_two[i].wait_recv()
            v1_hand[i + 2].start()

    by_core(v0_late, v1_late)

    r_one = own_rims(vol, vg, core)
    r_two = to_y(vg.at[rims, :, y, core], vg.at[rims, :, y, core])
    r_hand = hand([vg.at[rims, :, y_at(dy), core] for dy in (0, 3, 1, 2)])
    start(r_one)
    c0_one = [copy_of(cot, cg.at[mine, x_hi, y, 0], (s, flip))] + own_rims(cot, cg, 0)
    c0_two = to_y(cg.at[:, :, y, 0], cg.at[:, :, y, 0])
    c1_one = to_y(cot, cg.at[mine, x_hi, y, 1])
    c1_two = [copy_of(cg.at[mine, x_hi, :, 1], cg.at[mine, x_hi, :, 1], (s, flip))]
    c1_two += to_rims(
        (cg.at[edge_src, x_hi, :, 1], cg.at[pair_src, x_hi, :, 1]),
        (cg.at[edge_dst, x_hi, :, 1], cg.at[pair_dst, x_hi, :, 1]),
    )
    sems = shared_sems()
    c0_hand = hand([cg.at[:, :, y_at(dy), 0] for dy in (0, 3, 1, 2)], sems)
    c1_hand = hand(
        [
            cg.at[mine, x_hi, :, 1],
            cg.at[mine, 1 - x_hi, :, 1],
            cg.at[2 + x_lo, :, :, 1],
            cg.at[3 - x_lo, :, :, 1],
        ],
        sems,
    )
    by_core(lambda: start(c0_one), lambda: start(c1_one))

    pl.semaphore_wait(known_sem.at[1], 2)
    tell(2, 4)
    arrive(v0_hand)

    def cell_dot(lhs, plane):
        return lax.dot_general(
            lhs,
            vg[plane].reshape(256, 1024),
            (((1,), (1,)), ((), ())),
            preferred_element_type=jnp.float32,
        )

    term = cell_dot(cs[0:432, :], 0) + cell_dot(cs[144:576, :], 1)
    for half in range(2):
        for a in range(3):
            rows = term[144 * (2 - a) : 144 * (3 - a), 128 * half : 128 * half + 128]
            part[half, 18 * a : 18 * a + 18] = rows.reshape(18, 8, 128)
    part[:, 54:56] = jnp.zeros((2, 2, 8, 128), jnp.float32)
    quad[:, 7] = jnp.zeros((2, 8, 128), jnp.float32)

    r = z % 4
    zi = z // 4
    held = pl.ds((x_lo * 4 + r) * 7, 7)
    moves = [(2, True), (-2, False), (1, True), (-1, True), (1, False), (-1, False), (0, False)]
    n1 = []
    for half in range(2):
        n1.append([])
        for slot, (dz, same) in enumerate(moves):
            group = (x_lo if same else 1 - x_lo) * 4 + (r + dz + 4) % 4
            n1[half].append(
                send(part.at[half, pl.ds(group * 7, 7)], near.at[half, slot], (at(dz, same), c))
            )

    arrive(r_one)
    start(r_two)
    r_hand[0].start()

    pl.semaphore_wait(known_sem.at[2], 2)
    f1 = []
    for half in range(2):
        arrive(n1[half])
        total = part[half, held]
        for slot in range(7):
            total = total + near[half, slot]
        quad[half, 0:7] = total
        f1.append([])
        for slot, (step, dz) in enumerate(((2, 8), (1, 4), (3, -4))):
            tiles = pl.ds(2 * ((zi + step) % 4), 2)
            f1[half].append(send(quad.at[half, tiles], far.at[half, slot], (at(dz, True), c)))

    def c0_middle():
        arrive(c0_one)
        start(c0_two)
        c0_hand[0].start()

    def c1_middle():
        arrive(c1_one)
        start(c1_two)
        c1_hand[0].start()

    by_core(c0_middle, c1_middle)
    w1 = []
    for m in range(1, 16):
        to = lax.rem(c + m, 16)
        w1.append(send(kt.at[to], wr.at[:, c], (s, to)))

    def conv(weights, g, plane):
        order = (2, 0, 1) if plane == 0 else (0, 1, 3)
        total = None
        for taps_of, index in zip(weights, order):
            if index == 2:
                taps_of = jnp.where(low, jnp.zeros_like(taps_of), taps_of)
            if index == 3:
                taps_of = jnp.where(high, jnp.zeros_like(taps_of), taps_of)
            rows = g[index].reshape(256, 1024)
            product = jnp.dot(taps_of, rows, preferred_element_type=jnp.float32)
            total = product if total is None else total + product
        sums[...] = total

    for i in range(3):
        r_two[i].wait_recv()
        r_hand[i + 1].start()
    arrive(r_hand)
    forward = [ker_ref[9 * a : 9 * a + 9].reshape(144, 256) for a in range(3)]
    for plane in range(2):
        conv(forward, vg, plane)
        out_ref[plane] = tap_sum(sums, 1, column).reshape(16, 8, 128).astype(jnp.bfloat16)

    a1 = []
    chunk = pl.ds(2 * zi, 2)
    for half in range(2):
        arrive(f1[half])
        total = quad[half, chunk] + far[half, 0] + far[half, 1] + far[half, 2]
        own[half, chunk] = total * scale
        a1.append(
            [send(own.at[half, chunk], own.at[half, chunk], (at(dz, True), c)) for dz in (8, 4, -4)]
        )

    def c0_late():
        for i in range(3):
            c0_two[i].wait_recv()
            c0_hand[i + 1].start()

    def c1_late():
        c1_two[0].wait_recv()
        c1_hand[1].start()
        arrive(c1_two[1:3])
        c1_hand[2].start()
        arrive(c1_two[3:5])
        c1_hand[3].start()

    by_core(c0_late, c1_late)

    a2 = []
    for half in range(2):
        arrive(a1[half])
        full[half, held] = own[half, 0:7]
        for dz, same in moves:
            a2.append(send(own.at[half, pl.ds(0, 7)], full.at[half, held], (at(dz, same), c)))

    arrive(c0_hand)
    arrive(w1)
    last = wr[3].reshape(256, 128)
    backward = []
    for a in (2, 1, 0):
        lines = jnp.concatenate(
            [wr[a].reshape(256, 128), last[:, 16 * a : 16 * a + 16]], axis=1
        )
        backward.append(lines.T)
    for plane in range(2):
        conv(backward, cg, plane)
        inp_ref[plane] = tap_sum(sums, -1, column).reshape(16, 8, 128).astype(jnp.bfloat16)

    arrive(a2)
    for half in range(2):
        grad_ref[:, :, 128 * half : 128 * half + 128] = full[half, 0:54].reshape(27, 16, 128)

    by_core(
        lambda: ended(v0_one + v0_two + v0_hand + c0_one + c0_two + c0_hand),
        lambda: ended(v1_one + v1_two + v1_hand + c1_one + c1_two + c1_hand),
    )
    ended(r_one + r_two + r_hand + sent)


def on_device(volume, kernel, cotangent):
    depth, chans, height, width = volume.shape
    nspace = lax.axis_size("space")
    scale = 1.0 / math.sqrt(depth * nspace * height * width)
    vmem = pl.BlockSpec(memory_space=pltpu.VMEM)
    bf16, f32 = jnp.bfloat16, jnp.float32
    return pl.pallas_call(
        functools.partial(layer_kernel, nspace, scale),
        out_shape=(
            jax.ShapeDtypeStruct(volume.shape, bf16),
            jax.ShapeDtypeStruct(volume.shape, bf16),
            jax.ShapeDtypeStruct((27, 16, 256), f32),
        ),
        in_specs=[vmem] * 3,
        out_specs=(vmem,) * 3,
        scratch_shapes=[
            pltpu.VMEM((2, 16, 1024), bf16),
            pltpu.VMEM((2, 16, 1024), bf16),
            pltpu.VMEM((2, 16, 1024), bf16),
            pltpu.VMEM((4, 2, 4, 2, 16, 1024), bf16),
            pltpu.VMEM((4, 2, 4, 2, 16, 1024), bf16),
            pltpu.VMEM((16, 4, 16, 128), bf16),
            pltpu.VMEM((4, 16, 16, 128), bf16),
            pltpu.VMEM((576, 1024), bf16),
            pltpu.VMEM((144, 1024), f32),
            pltpu.VMEM((2, 56, 8, 128), f32),
            pltpu.VMEM((2, 7, 7, 8, 128), f32),
            pltpu.VMEM((2, 8, 8, 128), f32),
            pltpu.VMEM((2, 3, 2, 8, 128), f32),
            pltpu.VMEM((2, 8, 8, 128), f32),
            pltpu.VMEM((2, 56, 8, 128), f32),
            pltpu.SemaphoreType.DMA((COPIES,)),
            pltpu.SemaphoreType.DMA((COPIES,)),
            pltpu.SemaphoreType.REGULAR((3,)),
        ],
        compiler_params=pltpu.CompilerParams(
            collective_id=0, has_side_effects=True, vmem_limit_bytes=48 << 20
        ),
        name="layer",
    )(volume, cotangent, kernel)


def solution(mesh):
    return jax.shard_map(
        on_device,
        mesh=mesh,
        in_specs=(
            P("space", "chan", None, None),
            P(None, "chan", None),
            P("space", "chan", None, None),
        ),
        out_specs=(
            P("space", "chan", None, None),
            P("space", "chan", None, None),
            P(None, "chan", None),
        ),
        check_vma=False,
    )
```

time: 63.4 us -> 59.9 us (0.945)
  Pallas kernels: 58.2 us -> 54.4 us
  local copies, waits for them, and re-layouts: 3.83 us -> 4.63 us
    pallas_call x1, Pallas kernels: 58.2 us -> 54.4 us  [on_device(): pl.pallas_call(functools.partial(layer_kernel, nspace, scale), out_shape=...]
    unnamed x5 -> x9, local copies, waits for them, and re-layouts: 2.05 us -> 4.63 us
    reshape x2 -> x0, local copies, waits for them, and re-layouts: 1.79 us -> none  [the longest x1 0.91 us: on_device(): vol = volume.reshape(depth, chans, cells)]
where the time goes in v3:
time: 59.9 us; the launch traced here: 59.6 us
  Pallas kernels  54.4 us (91%)
  local copies, waits for them, and re-layouts  4.63 us (8%)
  between operations  0.65 us (1%)
    pallas_call x1, Pallas kernels, on_device(): pl.pallas_call(functools.partial(layer_kernel, nspace, scale), out_shape=...  54.4 us
    unnamed x9, local copies, waits for them, and re-layouts  4.63 us

profile of v3, /device:TPU:1, one launch (start us, length us, event | category | flops | bytes accessed | tf_op | source)
XLA Modules:
  0.0 59.6 jit_solution(5955903087813544633)
XLA Ops:
  0.6 0.0 copy-start
  0.6 0.9 %copy-done = bf16[27,16,256]{2,1,0:T(8,128)(2,1)S(1)} copy-done((bf16[27,16,256]{2,1,0:T(8,128)(2,1)S(1)}, bf16[27,16,256]{2,1,0:T(8,128)(2,1)}, u32[]{:S(2)}) %copy-start) | copy-done | bytes 221208
  1.6 0.0 copy-start.1
  1.6 0.8 %copy-done.1 = bf16[2,16,8,128]{3,2,1,0:T(8,128)(2,1)S(1)} copy-done((bf16[2,16,8,128]{3,2,1,0:T(8,128)(2,1)S(1)}, bf16[2,16,8,128]{3,2,1,0:T(8,128)(2,1)}, u32[]{:S(2)}) %copy-start.1) | copy-done | bytes 65560
  2.4 0.0 copy-start.2
  2.4 0.8 %copy-done.2 = bf16[2,16,8,128]{3,2,1,0:T(8,128)(2,1)S(1)} copy-done((bf16[2,16,8,128]{3,2,1,0:T(8,128)(2,1)S(1)}, bf16[2,16,8,128]{3,2,1,0:T(8,128)(2,1)}, u32[]{:S(2)}) %copy-start.2) | copy-done | bytes 65560
  3.2 54.4 %layer.1 = (bf16[2,16,8,128]{3,2,1,0:T(8,128)(2,1)S(1)}, bf16[2,16,8,128]{3,2,1,0:T(8,128)(2,1)S(1)}, f32[27,16,256]{2,1,0:T(8,128)S(1)}) custom-call(bf16[2,16,8,128]{3,2,1,0:T(8,128)(2,1)S(1)} %copy-done.1, bf16[2,16,8,128]{3,2,1,0:T(8,128)(2,1)S(1)} %copy-done.2, bf16[27,16,256]{2,1,0:T(8,128)(2,1)S(1)} %copy-done), custom_call_target="tpu_custom_call" | custom-call | tf_op jit(solution)/shard_map/layer/pallas_call | solution.py:435
  57.6 0.6 %copy.9 = bf16[2,16,8,128]{3,2,1,0:T(8,128)(2,1)} copy(bf16[2,16,8,128]{3,2,1,0:T(8,128)(2,1)S(1)} %get-tuple-element.6) | data formatting | bytes 131072
  58.3 0.6 %copy.10 = bf16[2,16,8,128]{3,2,1,0:T(8,128)(2,1)} copy(bf16[2,16,8,128]{3,2,1,0:T(8,128)(2,1)S(1)} %get-tuple-element.7) | data formatting | bytes 131072
  58.9 0.8 %copy.11 = f32[27,16,256]{2,1,0:T(8,128)} copy(f32[27,16,256]{2,1,0:T(8,128)S(1)} %get-tuple-element.8) | data formatting | bytes 884736
Async XLA Ops:
  0.6 0.9 %copy-start = (bf16[27,16,256]{2,1,0:T(8,128)(2,1)S(1)}, bf16[27,16,256]{2,1,0:T(8,128)(2,1)}, u32[]{:S(2)}) copy-start(bf16[27,16,256]{2,1,0:T(8,128)(2,1)} %ker_ref.1) | copy-start | bytes 663556
  1.6 0.8 %copy-start.1 = (bf16[2,16,8,128]{3,2,1,0:T(8,128)(2,1)S(1)}, bf16[2,16,8,128]{3,2,1,0:T(8,128)(2,1)}, u32[]{:S(2)}) copy-start(bf16[2,16,8,128]{3,2,1,0:T(8,128)(2,1)} %vol_ref.1) | copy-start | bytes 196612
  2.4 0.8 %copy-start.2 = (bf16[2,16,8,128]{3,2,1,0:T(8,128)(2,1)S(1)}, bf16[2,16,8,128]{3,2,1,0:T(8,128)(2,1)}, u32[]{:S(2)}) copy-start(bf16[2,16,8,128]{3,2,1,0:T(8,128)(2,1)} %cot_ref.1) | copy-start | bytes 196612

commit v4 on v3

--- a/solution.py
+++ b/solution.py
@@ -182,18 +182,32 @@
         count[0] += 4
         return list(range(count[0] - 4, count[0]))
 
-    v0_one = [copy_of(vol, vg.at[mine, x_hi, y, 0], (s, flip))]
-    v0_two = to_y(vg.at[mine, :, y, 0], vg.at[mine, :, y, 0])
-    v1_one = to_y(vol, vg.at[mine, x_hi, y, 1])
+    own_block = vg.at[mine, x_hi, y, core]
+    v_y = to_y(vol, own_block)
+    v_x = copy_of(vol, own_block, (s, flip))
+    start(v_y[0:2])
+    v_x.start()
+    v_y[2].start()
+    sides = (x_hi, 1 - x_hi)
+    steps = (0, 3, 1, 2)
+    hand_one = hand([vg.at[mine, sides[0], y_at(dy), core] for dy in steps])
+    hand_two = hand([vg.at[mine, sides[1], y_at(dy), core] for dy in steps])
+    sems = shared_sems()
+    v0_two = [
+        copy_of(
+            vg.at[mine, sides[1], y, 0], vg.at[mine, sides[1], y, 0], (s, chan_of(dy)), sems[i]
+        )
+        for i, dy in enumerate((1, 3, 2))
+    ]
     v1_two = [
-        copy_of(vg.at[p, x_hi, :, 1], vg.at[p, x_hi, :, 1], (s, flip)) for p in range(2)
+        copy_of(
+            vg.at[mine, sides[0], y_at(dy), 1],
+            vg.at[mine, sides[0], y_at(dy), 1],
+            (s, flip),
+            sems[i],
+        )
+        for i, dy in enumerate((3, 1, 2))
     ]
-    sems = shared_sems()
-    v0_hand = hand([vg.at[mine, :, y_at(dy), 0] for dy in (0, 3, 1, 2)], sems)
-    v1_hand = hand(
-        [vg.at[p, side, :, 1] for side in (x_hi, 1 - x_hi) for p in range(2)], sems
-    )
-    by_core(lambda: start(v0_one), lambda: start(v1_one))
     beside = [
         send(cot.at[edge_src], rim.at[edge_dst - 2], (edge, c)),
         send(cot.at[pair_src], rim.at[pair_dst - 2], (pair, c)),
@@ -214,29 +228,14 @@
     for plane in range(2):
         spread(cot[plane].astype(jnp.float32), plane + 1)
 
-    def v0_middle():
-        arrive(v0_one)
-        start(v0_two)
-        v0_hand[0].start()
-
-    def v1_middle():
-        arrive(v1_one)
-        start(v1_two)
-        start(v1_hand[0:2])
-
-    by_core(v0_middle, v1_middle)
-
-    taps = [ker_ref[t].astype(jnp.float32) for t in range(27)]
-    filler = jnp.zeros((16, 80), jnp.float32)
-    for to in range(16):
-        lanes = slice(16 * to, 16 * to + 16)
-        for a in range(3):
-            row = jnp.concatenate([taps[9 * a + t][:, lanes] for t in range(8)], axis=1)
-            kt[to, a] = row.astype(jnp.bfloat16)
-        row = jnp.concatenate([taps[9 * a + 8][:, lanes] for a in range(3)] + [filler], axis=1)
-        kt[to, 3] = row.astype(jnp.bfloat16)
-    wr[:, c] = kt[c]
-
+    hand_one[0].start()
+    v_x.wait_recv()
+    pl.when(core == 0)(lambda: start(v0_two))
+    hand_two[0].start()
+    for i in range(3):
+        v_y[i].wait_recv()
+        pl.when(core == 1)(v1_two[i].start)
+        hand_one[i + 1].start()
     pl.semaphore_wait(known_sem.at[0], 2)
     tell(1, 2)
     arrive(beside)
@@ -245,17 +244,42 @@
     spread(jnp.where(low, jnp.zeros_like(below), below), 0)
     spread(jnp.where(high, jnp.zeros_like(above), above), 3)
 
-    def v0_late():
-        for i in range(3):
-            v0_two[i].wait_recv()
-            v0_hand[i + 1].start()
-
-    def v1_late():
-        for i in range(2):
-            v1_two[i].wait_recv()
-            v1_hand[i + 2].start()
-
-    by_core(v0_late, v1_late)
+    pl.semaphore_wait(known_sem.at[1], 2)
+    arrive(hand_one)
+
+    def cell_dot(lhs, plane, half):
+        return lax.dot_general(
+            lhs,
+            vg[plane, sides[half]].reshape(128, 1024),
+            (((1,), (1,)), ((), ())),
+            preferred_element_type=jnp.float32,
+        )
+
+    r = z % 4
+    zi = z // 4
+    held = pl.ds((x_lo * 4 + r) * 7, 7)
+    moves = [(2, True), (-2, False), (1, True), (-1, True), (1, False), (-1, False), (0, False)]
+    n1 = []
+
+    def reduce_near(half):
+        term = cell_dot(cs[0:432, :], 0, half) + cell_dot(cs[144:576, :], 1, half)
+        for a in range(3):
+            rows = term[144 * (2 - a) : 144 * (3 - a)]
+            part[half, 18 * a : 18 * a + 18] = rows.reshape(18, 8, 128)
+        part[half, 54:56] = jnp.zeros((2, 8, 128), jnp.float32)
+        n1.append([])
+        for slot, (dz, same) in enumerate(moves):
+            group = (x_lo if same else 1 - x_lo) * 4 + (r + dz + 4) % 4
+            n1[half].append(
+                send(part.at[half, pl.ds(group * 7, 7)], near.at[half, slot], (at(dz, same), c))
+            )
+
+    reduce_near(0)
+
+    for i in range(3):
+        pl.when(core == 0)(v0_two[i].wait_recv)
+        pl.when(core == 1)(v1_two[i].wait_recv)
+        hand_two[i + 1].start()
 
     r_one = own_rims(vol, vg, core)
     r_two = to_y(vg.at[rims, :, y, core], vg.at[rims, :, y, core])
@@ -282,55 +306,26 @@
     )
     by_core(lambda: start(c0_one), lambda: start(c1_one))
 
-    pl.semaphore_wait(known_sem.at[1], 2)
-    tell(2, 4)
-    arrive(v0_hand)
-
-    def cell_dot(lhs, plane):
-        return lax.dot_general(
-            lhs,
-            vg[plane].reshape(256, 1024),
-            (((1,), (1,)), ((), ())),
-            preferred_element_type=jnp.float32,
-        )
-
-    term = cell_dot(cs[0:432, :], 0) + cell_dot(cs[144:576, :], 1)
-    for half in range(2):
-        for a in range(3):
-            rows = term[144 * (2 - a) : 144 * (3 - a), 128 * half : 128 * half + 128]
-            part[half, 18 * a : 18 * a + 18] = rows.reshape(18, 8, 128)
-    part[:, 54:56] = jnp.zeros((2, 2, 8, 128), jnp.float32)
-    quad[:, 7] = jnp.zeros((2, 8, 128), jnp.float32)
-
-    r = z % 4
-    zi = z // 4
-    held = pl.ds((x_lo * 4 + r) * 7, 7)
-    moves = [(2, True), (-2, False), (1, True), (-1, True), (1, False), (-1, False), (0, False)]
-    n1 = []
-    for half in range(2):
-        n1.append([])
-        for slot, (dz, same) in enumerate(moves):
-            group = (x_lo if same else 1 - x_lo) * 4 + (r + dz + 4) % 4
-            n1[half].append(
-                send(part.at[half, pl.ds(group * 7, 7)], near.at[half, slot], (at(dz, same), c))
-            )
+    arrive(hand_two)
+    reduce_near(1)
 
     arrive(r_one)
     start(r_two)
     r_hand[0].start()
 
-    pl.semaphore_wait(known_sem.at[2], 2)
+    hop = [at(4 * (1 - 2 * ((zi + r + i) % 2)), True) for i in range(2)]
+
+    def exchange(half, step):
+        return send(quad.at[half, step], far.at[half, step], (hop[(half + step) % 2], c))
+
     f1 = []
     for half in range(2):
         arrive(n1[half])
         total = part[half, held]
         for slot in range(7):
             total = total + near[half, slot]
-        quad[half, 0:7] = total
-        f1.append([])
-        for slot, (step, dz) in enumerate(((2, 8), (1, 4), (3, -4))):
-            tiles = pl.ds(2 * ((zi + step) % 4), 2)
-            f1[half].append(send(quad.at[half, tiles], far.at[half, slot], (at(dz, True), c)))
+        quad[half, 0] = total
+        f1.append(exchange(half, 0))
 
     def c0_middle():
         arrive(c0_one)
@@ -343,6 +338,17 @@
         c1_hand[0].start()
 
     by_core(c0_middle, c1_middle)
+    taps = [ker_ref[t].astype(jnp.float32) for t in range(27)]
+    filler = jnp.zeros((16, 80), jnp.float32)
+    for to in range(16):
+        lanes = slice(16 * to, 16 * to + 16)
+        for a in range(3):
+            row = jnp.concatenate([taps[9 * a + t][:, lanes] for t in range(8)], axis=1)
+            kt[to, a] = row.astype(jnp.bfloat16)
+        row = jnp.concatenate([taps[9 * a + 8][:, lanes] for a in range(3)] + [filler], axis=1)
+        kt[to, 3] = row.astype(jnp.bfloat16)
+    wr[:, c] = kt[c]
+
     w1 = []
     for m in range(1, 16):
         to = lax.rem(c + m, 16)
@@ -361,6 +367,12 @@
             total = product if total is None else total + product
         sums[...] = total
 
+    f2 = []
+    for half in range(2):
+        f1[half].wait_recv()
+        quad[half, 1] = quad[half, 0] + far[half, 0]
+        f2.append(exchange(half, 1))
+
     for i in range(3):
         r_two[i].wait_recv()
         r_hand[i + 1].start()
@@ -370,15 +382,14 @@
         conv(forward, vg, plane)
         out_ref[plane] = tap_sum(sums, 1, column).reshape(16, 8, 128).astype(jnp.bfloat16)
 
-    a1 = []
-    chunk = pl.ds(2 * zi, 2)
+    a2 = []
     for half in range(2):
-        arrive(f1[half])
-        total = quad[half, chunk] + far[half, 0] + far[half, 1] + far[half, 2]
-        own[half, chunk] = total * scale
-        a1.append(
-            [send(own.at[half, chunk], own.at[half, chunk], (at(dz, True), c)) for dz in (8, 4, -4)]
-        )
+        f2[half].wait_recv()
+        total = (quad[half, 1] + far[half, 1]) * scale
+        own[half] = total
+        full[half, held] = total
+        for dz, same in moves:
+            a2.append(send(own.at[half], full.at[half, held], (at(dz, same), c)))
 
     def c0_late():
         for i in range(3):
@@ -395,13 +406,6 @@
 
     by_core(c0_late, c1_late)
 
-    a2 = []
-    for half in range(2):
-        arrive(a1[half])
-        full[half, held] = own[half, 0:7]
-        for dz, same in moves:
-            a2.append(send(own.at[half, pl.ds(0, 7)], full.at[half, held], (at(dz, same), c)))
-
     arrive(c0_hand)
     arrive(w1)
     last = wr[3].reshape(256, 128)
@@ -417,13 +421,14 @@
 
     arrive(a2)
     for half in range(2):
-        grad_ref[:, :, 128 * half : 128 * half + 128] = full[half, 0:54].reshape(27, 16, 128)
+        lanes = pl.ds(pl.multiple_of(128 * sides[half], 128), 128)
+        grad_ref[:, :, lanes] = full[half, 0:54].reshape(27, 16, 128)
 
     by_core(
-        lambda: ended(v0_one + v0_two + v0_hand + c0_one + c0_two + c0_hand),
-        lambda: ended(v1_one + v1_two + v1_hand + c1_one + c1_two + c1_hand),
+        lambda: ended(v0_two + c0_one + c0_two + c0_hand),
+        lambda: ended(v1_two + c1_one + c1_two + c1_hand),
     )
-    ended(r_one + r_two + r_hand + sent)
+    ended(v_y + [v_x] + hand_one + hand_two + r_one + r_two + r_hand + sent)
 
 
 def on_device(volume, kernel, cotangent):
@@ -453,13 +458,13 @@
             pltpu.VMEM((144, 1024), f32),
             pltpu.VMEM((2, 56, 8, 128), f32),
             pltpu.VMEM((2, 7, 7, 8, 128), f32),
-            pltpu.VMEM((2, 8, 8, 128), f32),
-            pltpu.VMEM((2, 3, 2, 8, 128), f32),
-            pltpu.VMEM((2, 8, 8, 128), f32),
+            pltpu.VMEM((2, 2, 7, 8, 128), f32),
+            pltpu.VMEM((2, 2, 7, 8, 128), f32),
+            pltpu.VMEM((2, 7, 8, 128), f32),
             pltpu.VMEM((2, 56, 8, 128), f32),
             pltpu.SemaphoreType.DMA((COPIES,)),
             pltpu.SemaphoreType.DMA((COPIES,)),
-            pltpu.SemaphoreType.REGULAR((3,)),
+            pltpu.SemaphoreType.REGULAR((2,)),
         ],
         compiler_params=pltpu.CompilerParams(
             collective_id=0, has_side_effects=True, vmem_limit_bytes=48 << 20

time: 59.9 us -> 54.8 us (0.915)
  Pallas kernels: 54.4 us -> 49.3 us
    pallas_call x1, Pallas kernels: 54.4 us -> 49.3 us  [on_device(): pl.pallas_call(functools.partial(layer_kernel, nspace, scale), out_shape=...]
where the time goes in v4:
time: 54.8 us; the launch traced here: 54.6 us
  Pallas kernels  49.3 us (90%)
  local copies, waits for them, and re-layouts  4.63 us (8%)
  between operations  0.65 us (1%)
    pallas_call x1, Pallas kernels, on_device(): pl.pallas_call(functools.partial(layer_kernel, nspace, scale), out_shape=...  49.3 us
    unnamed x9, local copies, waits for them, and re-layouts  4.63 us

profile of v4, /device:TPU:1, one launch (start us, length us, event | category | flops | bytes accessed | tf_op | source)
XLA Modules:
  0.0 54.6 jit_solution(12849995587984361028)
XLA Ops:
  0.6 0.0 copy-start
  0.6 0.9 %copy-done = bf16[27,16,256]{2,1,0:T(8,128)(2,1)S(1)} copy-done((bf16[27,16,256]{2,1,0:T(8,128)(2,1)S(1)}, bf16[27,16,256]{2,1,0:T(8,128)(2,1)}, u32[]{:S(2)}) %copy-start) | copy-done | bytes 221208
  1.6 0.0 copy-start.1
  1.6 0.8 %copy-done.1 = bf16[2,16,8,128]{3,2,1,0:T(8,128)(2,1)S(1)} copy-done((bf16[2,16,8,128]{3,2,1,0:T(8,128)(2,1)S(1)}, bf16[2,16,8,128]{3,2,1,0:T(8,128)(2,1)}, u32[]{:S(2)}) %copy-start.1) | copy-done | bytes 65560
  2.4 0.0 copy-start.2
  2.4 0.8 %copy-done.2 = bf16[2,16,8,128]{3,2,1,0:T(8,128)(2,1)S(1)} copy-done((bf16[2,16,8,128]{3,2,1,0:T(8,128)(2,1)S(1)}, bf16[2,16,8,128]{3,2,1,0:T(8,128)(2,1)}, u32[]{:S(2)}) %copy-start.2) | copy-done | bytes 65560
  3.2 49.3 %layer.1 = (bf16[2,16,8,128]{3,2,1,0:T(8,128)(2,1)S(1)}, bf16[2,16,8,128]{3,2,1,0:T(8,128)(2,1)S(1)}, f32[27,16,256]{2,1,0:T(8,128)S(1)}) custom-call(bf16[2,16,8,128]{3,2,1,0:T(8,128)(2,1)S(1)} %copy-done.1, bf16[2,16,8,128]{3,2,1,0:T(8,128)(2,1)S(1)} %copy-done.2, bf16[27,16,256]{2,1,0:T(8,128)(2,1)S(1)} %copy-done), custom_call_target="tpu_custom_call" | custom-call | tf_op jit(solution)/shard_map/layer/pallas_call | solution.py:440
  52.5 0.6 %copy.9 = bf16[2,16,8,128]{3,2,1,0:T(8,128)(2,1)} copy(bf16[2,16,8,128]{3,2,1,0:T(8,128)(2,1)S(1)} %get-tuple-element.6) | data formatting | bytes 131072
  53.2 0.6 %copy.10 = bf16[2,16,8,128]{3,2,1,0:T(8,128)(2,1)} copy(bf16[2,16,8,128]{3,2,1,0:T(8,128)(2,1)S(1)} %get-tuple-element.7) | data formatting | bytes 131072
  53.8 0.8 %copy.11 = f32[27,16,256]{2,1,0:T(8,128)} copy(f32[27,16,256]{2,1,0:T(8,128)S(1)} %get-tuple-element.8) | data formatting | bytes 884736
Async XLA Ops:
  0.6 0.9 %copy-start = (bf16[27,16,256]{2,1,0:T(8,128)(2,1)S(1)}, bf16[27,16,256]{2,1,0:T(8,128)(2,1)}, u32[]{:S(2)}) copy-start(bf16[27,16,256]{2,1,0:T(8,128)(2,1)} %ker_ref.1) | copy-start | bytes 663556
  1.6 0.8 %copy-start.1 = (bf16[2,16,8,128]{3,2,1,0:T(8,128)(2,1)S(1)}, bf16[2,16,8,128]{3,2,1,0:T(8,128)(2,1)}, u32[]{:S(2)}) copy-start(bf16[2,16,8,128]{3,2,1,0:T(8,128)(2,1)} %vol_ref.1) | copy-start | bytes 196612
  2.4 0.8 %copy-start.2 = (bf16[2,16,8,128]{3,2,1,0:T(8,128)(2,1)S(1)}, bf16[2,16,8,128]{3,2,1,0:T(8,128)(2,1)}, u32[]{:S(2)}) copy-start(bf16[2,16,8,128]{3,2,1,0:T(8,128)(2,1)} %cot_ref.1) | copy-start | bytes 196612

commit v5 on v4

--- a/solution.py
+++ b/solution.py
@@ -54,6 +54,7 @@
     out_ref,
     inp_ref,
     grad_ref,
+    rows,
     vol,
     cot,
     rim,
@@ -102,13 +103,12 @@
     for peer in peers:
         pl.semaphore_signal(barrier, inc=1, device_id=peer, device_id_type=MESH)
 
-    for plane in range(2):
-        block = vol_ref[plane].astype(jnp.float32).reshape(16, 1024)
-        vol[plane] = block.astype(jnp.bfloat16)
-        vg[plane, x_hi, y, core] = block.astype(jnp.bfloat16)
-        block = cot_ref[plane].astype(jnp.float32).reshape(16, 1024)
-        cot[plane] = block.astype(jnp.bfloat16)
-        cg[plane, x_hi, y, core] = block.astype(jnp.bfloat16)
+    for ref, flat in ((vol_ref, vol), (cot_ref, cot)):
+        for plane in range(2):
+            rows[plane] = ref[plane].astype(jnp.float32).reshape(128, 128)
+            for h in range(8):
+                line = rows[plane, pl.ds(h, 16, stride=8), :].astype(jnp.bfloat16)
+                flat[plane, :, 128 * h : 128 * h + 128] = line
     pl.semaphore_wait(barrier, len(peers))
 
     count = [0]
@@ -188,6 +188,10 @@
     start(v_y[0:2])
     v_x.start()
     v_y[2].start()
+    r_one = own_rims(vol, vg, core)
+    start(r_one)
+    vg[0:2, x_hi, y, core] = vol[...]
+    cg[0:2, x_hi, y, core] = cot[...]
     sides = (x_hi, 1 - x_hi)
     steps = (0, 3, 1, 2)
     hand_one = hand([vg.at[mine, sides[0], y_at(dy), core] for dy in steps])
@@ -281,10 +285,8 @@
         pl.when(core == 1)(v1_two[i].wait_recv)
         hand_two[i + 1].start()
 
-    r_one = own_rims(vol, vg, core)
     r_two = to_y(vg.at[rims, :, y, core], vg.at[rims, :, y, core])
     r_hand = hand([vg.at[rims, :, y_at(dy), core] for dy in (0, 3, 1, 2)])
-    start(r_one)
     c0_one = [copy_of(cot, cg.at[mine, x_hi, y, 0], (s, flip))] + own_rims(cot, cg, 0)
     c0_two = to_y(cg.at[:, :, y, 0], cg.at[:, :, y, 0])
     c1_one = to_y(cot, cg.at[mine, x_hi, y, 1])
@@ -304,14 +306,12 @@
         ],
         sems,
     )
-    by_core(lambda: start(c0_one), lambda: start(c1_one))
-
     arrive(hand_two)
     reduce_near(1)
-
     arrive(r_one)
     start(r_two)
     r_hand[0].start()
+    by_core(lambda: start(c0_one), lambda: start(c1_one))
 
     hop = [at(4 * (1 - 2 * ((zi + r + i) % 2)), True) for i in range(2)]
 
@@ -373,6 +373,15 @@
         quad[half, 1] = quad[half, 0] + far[half, 0]
         f2.append(exchange(half, 1))
 
+    a2 = []
+    for half in range(2):
+        f2[half].wait_recv()
+        total = (quad[half, 1] + far[half, 1]) * scale
+        own[half] = total
+        full[half, held] = total
+        for dz, same in moves:
+            a2.append(send(own.at[half], full.at[half, held], (at(dz, same), c)))
+
     for i in range(3):
         r_two[i].wait_recv()
         r_hand[i + 1].start()
@@ -381,15 +390,6 @@
     for plane in range(2):
         conv(forward, vg, plane)
         out_ref[plane] = tap_sum(sums, 1, column).reshape(16, 8, 128).astype(jnp.bfloat16)
-
-    a2 = []
-    for half in range(2):
-        f2[half].wait_recv()
-        total = (quad[half, 1] + far[half, 1]) * scale
-        own[half] = total
-        full[half, held] = total
-        for dz, same in moves:
-            a2.append(send(own.at[half], full.at[half, held], (at(dz, same), c)))
 
     def c0_late():
         for i in range(3):
@@ -431,13 +431,22 @@
     ended(v_y + [v_x] + hand_one + hand_two + r_one + r_two + r_hand + sent)
 
 
+def store_kernel(a_ref, b_ref, c_ref, a_out, b_out, c_out, sem):
+    pairs = ((c_ref, c_out), (a_ref, a_out), (b_ref, b_out))
+    copies = [pltpu.make_async_copy(x, y, sem.at[i]) for i, (x, y) in enumerate(pairs)]
+    for copy in copies:
+        copy.start()
+    for copy in copies:
+        copy.wait()
+
+
 def on_device(volume, kernel, cotangent):
     depth, chans, height, width = volume.shape
     nspace = lax.axis_size("space")
     scale = 1.0 / math.sqrt(depth * nspace * height * width)
     vmem = pl.BlockSpec(memory_space=pltpu.VMEM)
     bf16, f32 = jnp.bfloat16, jnp.float32
-    return pl.pallas_call(
+    results = pl.pallas_call(
         functools.partial(layer_kernel, nspace, scale),
         out_shape=(
             jax.ShapeDtypeStruct(volume.shape, bf16),
@@ -447,6 +456,7 @@
         in_specs=[vmem] * 3,
         out_specs=(vmem,) * 3,
         scratch_shapes=[
+            pltpu.VMEM((2, 128, 128), f32),
             pltpu.VMEM((2, 16, 1024), bf16),
             pltpu.VMEM((2, 16, 1024), bf16),
             pltpu.VMEM((2, 16, 1024), bf16),
@@ -471,6 +481,15 @@
         ),
         name="layer",
     )(volume, cotangent, kernel)
+    return pl.pallas_call(
+        store_kernel,
+        out_shape=tuple(jax.ShapeDtypeStruct(x.shape, x.dtype) for x in results),
+        in_specs=[vmem] * 3,
+        out_specs=(pl.BlockSpec(memory_space=pltpu.HBM),) * 3,
+        scratch_shapes=[pltpu.SemaphoreType.DMA((3,))],
+        compiler_params=pltpu.CompilerParams(vmem_limit_bytes=8 << 20),
+        name="store",
+    )(*results)
 
 
 def solution(mesh):

time: 54.8 us -> 56.9 us (1.038)
  Pallas kernels: 49.3 us -> 53.4 us
  local copies, waits for them, and re-layouts: 4.63 us -> 2.61 us
    pallas_call x1, Pallas kernels: 49.3 us -> 52.5 us  [on_device(): pl.pallas_call(functools.partial(layer_kernel, nspace, scale), out_shape=...]
    unnamed x9 -> x6, local copies, waits for them, and re-layouts: 4.63 us -> 2.61 us
    pallas_call x0 -> x1, Pallas kernels: none -> 0.82 us  [on_device(): pl.pallas_call(store_kernel, out_shape=tuple((jax.ShapeDtypeStruct(x.shap...]
where the time goes in v5:
time: 56.9 us; the launch traced here: 56.6 us
  Pallas kernels  53.4 us (94%)
  local copies, waits for them, and re-layouts  2.61 us (5%)
  between operations  0.65 us (1%)
    pallas_call x1, Pallas kernels, on_device(): pl.pallas_call(functools.partial(layer_kernel, nspace, scale), out_shape=...  52.5 us
    unnamed x6, local copies, waits for them, and re-layouts  2.61 us

profile of v5, /device:TPU:1, one launch (start us, length us, event | category | flops | bytes accessed | tf_op | source)
XLA Modules:
  0.0 56.6 jit_solution(3628513573939892698)
XLA Ops:
  0.6 0.0 copy-start
  0.6 0.9 %copy-done = bf16[27,16,256]{2,1,0:T(8,128)(2,1)S(1)} copy-done((bf16[27,16,256]{2,1,0:T(8,128)(2,1)S(1)}, bf16[27,16,256]{2,1,0:T(8,128)(2,1)}, u32[]{:S(2)}) %copy-start) | copy-done | bytes 221208
  1.6 0.0 copy-start.1
  1.6 0.8 %copy-done.1 = bf16[2,16,8,128]{3,2,1,0:T(8,128)(2,1)S(1)} copy-done((bf16[2,16,8,128]{3,2,1,0:T(8,128)(2,1)S(1)}, bf16[2,16,8,128]{3,2,1,0:T(8,128)(2,1)}, u32[]{:S(2)}) %copy-start.1) | copy-done | bytes 65560
  2.4 0.0 copy-start.2
  2.4 0.8 %copy-done.2 = bf16[2,16,8,128]{3,2,1,0:T(8,128)(2,1)S(1)} copy-done((bf16[2,16,8,128]{3,2,1,0:T(8,128)(2,1)S(1)}, bf16[2,16,8,128]{3,2,1,0:T(8,128)(2,1)}, u32[]{:S(2)}) %copy-start.2) | copy-done | bytes 65560
  3.2 52.5 %layer.1 = (bf16[2,16,8,128]{3,2,1,0:T(8,128)(2,1)S(1)}, bf16[2,16,8,128]{3,2,1,0:T(8,128)(2,1)S(1)}, f32[27,16,256]{2,1,0:T(8,128)S(1)}) custom-call(bf16[2,16,8,128]{3,2,1,0:T(8,128)(2,1)S(1)} %copy-done.1, bf16[2,16,8,128]{3,2,1,0:T(8,128)(2,1)S(1)} %copy-done.2, bf16[27,16,256]{2,1,0:T(8,128)(2,1)S(1)} %copy-done), custom_call_target="tpu_custom_call" | custom-call | tf_op jit(solution)/shard_map/layer/pallas_call | solution.py:449
  55.8 0.8 %store.1 = (bf16[2,16,8,128]{3,2,1,0:T(8,128)(2,1)}, bf16[2,16,8,128]{3,2,1,0:T(8,128)(2,1)}, f32[27,16,256]{2,1,0:T(8,128)}) custom-call(bf16[2,16,8,128]{3,2,1,0:T(8,128)(2,1)S(1)} %get-tuple-element.6.a_ref, bf16[2,16,8,128]{3,2,1,0:T(8,128)(2,1)S(1)} %get-tuple-element.7.b_ref, f32[27,16,256]{2,1,0:T(8,128)S(1)} %get-tuple-element.8.c_ref), custom_call_target="tpu_custom_call" | custom-call | tf_op jit(solution)/shard_map/store/pallas_call | solution.py:484
Async XLA Ops:
  0.6 0.9 %copy-start = (bf16[27,16,256]{2,1,0:T(8,128)(2,1)S(1)}, bf16[27,16,256]{2,1,0:T(8,128)(2,1)}, u32[]{:S(2)}) copy-start(bf16[27,16,256]{2,1,0:T(8,128)(2,1)} %ker_ref.1) | copy-start | bytes 663556
  1.6 0.8 %copy-start.1 = (bf16[2,16,8,128]{3,2,1,0:T(8,128)(2,1)S(1)}, bf16[2,16,8,128]{3,2,1,0:T(8,128)(2,1)}, u32[]{:S(2)}) copy-start(bf16[2,16,8,128]{3,2,1,0:T(8,128)(2,1)} %vol_ref.1) | copy-start | bytes 196612
  2.4 0.8 %copy-start.2 = (bf16[2,16,8,128]{3,2,1,0:T(8,128)(2,1)S(1)}, bf16[2,16,8,128]{3,2,1,0:T(8,128)(2,1)}, u32[]{:S(2)}) copy-start(bf16[2,16,8,128]{3,2,1,0:T(8,128)(2,1)} %cot_ref.1) | copy-start | bytes 196612

commit v6 on v5

--- a/solution.py
+++ b/solution.py
@@ -188,8 +188,6 @@
     start(v_y[0:2])
     v_x.start()
     v_y[2].start()
-    r_one = own_rims(vol, vg, core)
-    start(r_one)
     vg[0:2, x_hi, y, core] = vol[...]
     cg[0:2, x_hi, y, core] = cot[...]
     sides = (x_hi, 1 - x_hi)
@@ -285,6 +283,7 @@
         pl.when(core == 1)(v1_two[i].wait_recv)
         hand_two[i + 1].start()
 
+    r_one = own_rims(vol, vg, core)
     r_two = to_y(vg.at[rims, :, y, core], vg.at[rims, :, y, core])
     r_hand = hand([vg.at[rims, :, y_at(dy), core] for dy in (0, 3, 1, 2)])
     c0_one = [copy_of(cot, cg.at[mine, x_hi, y, 0], (s, flip))] + own_rims(cot, cg, 0)
@@ -306,12 +305,13 @@
         ],
         sems,
     )
+    start(r_one)
+    by_core(lambda: start(c0_one), lambda: start(c1_one))
     arrive(hand_two)
     reduce_near(1)
     arrive(r_one)
     start(r_two)
     r_hand[0].start()
-    by_core(lambda: start(c0_one), lambda: start(c1_one))
 
     hop = [at(4 * (1 - 2 * ((zi + r + i) % 2)), True) for i in range(2)]
 

time: 56.9 us -> 53.9 us (0.947)
  Pallas kernels: 53.4 us -> 50.4 us
    pallas_call x1, Pallas kernels: 52.5 us -> 49.6 us  [on_device(): pl.pallas_call(functools.partial(layer_kernel, nspace, scale), out_shape=...]
where the time goes in v6:
time: 53.9 us; the launch traced here: 53.6 us
  Pallas kernels  50.4 us (94%)
  local copies, waits for them, and re-layouts  2.61 us (5%)
  between operations  0.65 us (1%)
    pallas_call x1, Pallas kernels, on_device(): pl.pallas_call(functools.partial(layer_kernel, nspace, scale), out_shape=...  49.6 us
    unnamed x6, local copies, waits for them, and re-layouts  2.61 us

profile of v6, /device:TPU:1, one launch (start us, length us, event | category | flops | bytes accessed | tf_op | source)
XLA Modules:
  0.0 53.6 jit_solution(8642099396750005503)
XLA Ops:
  0.6 0.0 copy-start
  0.6 0.9 %copy-done = bf16[27,16,256]{2,1,0:T(8,128)(2,1)S(1)} copy-done((bf16[27,16,256]{2,1,0:T(8,128)(2,1)S(1)}, bf16[27,16,256]{2,1,0:T(8,128)(2,1)}, u32[]{:S(2)}) %copy-start) | copy-done | bytes 221208
  1.6 0.0 copy-start.1
  1.6 0.8 %copy-done.1 = bf16[2,16,8,128]{3,2,1,0:T(8,128)(2,1)S(1)} copy-done((bf16[2,16,8,128]{3,2,1,0:T(8,128)(2,1)S(1)}, bf16[2,16,8,128]{3,2,1,0:T(8,128)(2,1)}, u32[]{:S(2)}) %copy-start.1) | copy-done | bytes 65560
  2.4 0.0 copy-start.2
  2.4 0.8 %copy-done.2 = bf16[2,16,8,128]{3,2,1,0:T(8,128)(2,1)S(1)} copy-done((bf16[2,16,8,128]{3,2,1,0:T(8,128)(2,1)S(1)}, bf16[2,16,8,128]{3,2,1,0:T(8,128)(2,1)}, u32[]{:S(2)}) %copy-start.2) | copy-done | bytes 65560
  3.2 49.6 %layer.1 = (bf16[2,16,8,128]{3,2,1,0:T(8,128)(2,1)S(1)}, bf16[2,16,8,128]{3,2,1,0:T(8,128)(2,1)S(1)}, f32[27,16,256]{2,1,0:T(8,128)S(1)}) custom-call(bf16[2,16,8,128]{3,2,1,0:T(8,128)(2,1)S(1)} %copy-done.1, bf16[2,16,8,128]{3,2,1,0:T(8,128)(2,1)S(1)} %copy-done.2, bf16[27,16,256]{2,1,0:T(8,128)(2,1)S(1)} %copy-done), custom_call_target="tpu_custom_call" | custom-call | tf_op jit(solution)/shard_map/layer/pallas_call | solution.py:449
  52.8 0.8 %store.1 = (bf16[2,16,8,128]{3,2,1,0:T(8,128)(2,1)}, bf16[2,16,8,128]{3,2,1,0:T(8,128)(2,1)}, f32[27,16,256]{2,1,0:T(8,128)}) custom-call(bf16[2,16,8,128]{3,2,1,0:T(8,128)(2,1)S(1)} %get-tuple-element.6.a_ref, bf16[2,16,8,128]{3,2,1,0:T(8,128)(2,1)S(1)} %get-tuple-element.7.b_ref, f32[27,16,256]{2,1,0:T(8,128)S(1)} %get-tuple-element.8.c_ref), custom_call_target="tpu_custom_call" | custom-call | tf_op jit(solution)/shard_map/store/pallas_call | solution.py:484
Async XLA Ops:
  0.6 0.9 %copy-start = (bf16[27,16,256]{2,1,0:T(8,128)(2,1)S(1)}, bf16[27,16,256]{2,1,0:T(8,128)(2,1)}, u32[]{:S(2)}) copy-start(bf16[27,16,256]{2,1,0:T(8,128)(2,1)} %ker_ref.1) | copy-start | bytes 663556
  1.6 0.8 %copy-start.1 = (bf16[2,16,8,128]{3,2,1,0:T(8,128)(2,1)S(1)}, bf16[2,16,8,128]{3,2,1,0:T(8,128)(2,1)}, u32[]{:S(2)}) copy-start(bf16[2,16,8,128]{3,2,1,0:T(8,128)(2,1)} %vol_ref.1) | copy-start | bytes 196612
  2.4 0.8 %copy-start.2 = (bf16[2,16,8,128]{3,2,1,0:T(8,128)(2,1)S(1)}, bf16[2,16,8,128]{3,2,1,0:T(8,128)(2,1)}, u32[]{:S(2)}) copy-start(bf16[2,16,8,128]{3,2,1,0:T(8,128)(2,1)} %cot_ref.1) | copy-start | bytes 196612

commit v7 on v6

--- a/solution.py
+++ b/solution.py
@@ -48,12 +48,14 @@
 def layer_kernel(
     nspace,
     scale,
-    vol_ref,
-    cot_ref,
-    ker_ref,
+    vol_hbm,
+    cot_hbm,
+    ker_hbm,
     out_ref,
     inp_ref,
     grad_ref,
+    blocks,
+    ker_ref,
     rows,
     vol,
     cot,
@@ -73,6 +75,7 @@
     send_sem,
     recv_sem,
     known_sem,
+    load_sem,
 ):
     s = lax.axis_index("space")
     c = lax.axis_index("chan")
@@ -103,9 +106,17 @@
     for peer in peers:
         pl.semaphore_signal(barrier, inc=1, device_id=peer, device_id_type=MESH)
 
-    for ref, flat in ((vol_ref, vol), (cot_ref, cot)):
+    loads = [
+        pltpu.make_async_copy(vol_hbm, blocks.at[0], load_sem.at[0]),
+        pltpu.make_async_copy(cot_hbm, blocks.at[1], load_sem.at[1]),
+        pltpu.make_async_copy(ker_hbm, ker_ref, load_sem.at[2]),
+    ]
+    for load in loads:
+        load.start()
+    for k, flat in enumerate((vol, cot)):
+        loads[k].wait()
         for plane in range(2):
-            rows[plane] = ref[plane].astype(jnp.float32).reshape(128, 128)
+            rows[plane] = blocks[k, plane].astype(jnp.float32).reshape(128, 128)
             for h in range(8):
                 line = rows[plane, pl.ds(h, 16, stride=8), :].astype(jnp.bfloat16)
                 flat[plane, :, 128 * h : 128 * h + 128] = line
@@ -338,6 +349,7 @@
         c1_hand[0].start()
 
     by_core(c0_middle, c1_middle)
+    loads[2].wait()
     taps = [ker_ref[t].astype(jnp.float32) for t in range(27)]
     filler = jnp.zeros((16, 80), jnp.float32)
     for to in range(16):
@@ -431,13 +443,17 @@
     ended(v_y + [v_x] + hand_one + hand_two + r_one + r_two + r_hand + sent)
 
 
-def store_kernel(a_ref, b_ref, c_ref, a_out, b_out, c_out, sem):
-    pairs = ((c_ref, c_out), (a_ref, a_out), (b_ref, b_out))
-    copies = [pltpu.make_async_copy(x, y, sem.at[i]) for i, (x, y) in enumerate(pairs)]
-    for copy in copies:
-        copy.start()
-    for copy in copies:
-        copy.wait()
+def store_kernel(a_ref, b_ref, c_ref, a_out, b_out, c_out, a, b, c, sem):
+    parts = ((c_ref, c, c_out), (a_ref, a, a_out), (b_ref, b, b_out))
+    loads = [pltpu.make_async_copy(x, v, sem.at[i]) for i, (x, v, y) in enumerate(parts)]
+    stores = [pltpu.make_async_copy(v, y, sem.at[i + 3]) for i, (x, v, y) in enumerate(parts)]
+    for load in loads:
+        load.start()
+    for load, store in zip(loads, stores):
+        load.wait()
+        store.start()
+    for store in stores:
+        store.wait()
 
 
 def on_device(volume, kernel, cotangent):
@@ -453,9 +469,11 @@
             jax.ShapeDtypeStruct(volume.shape, bf16),
             jax.ShapeDtypeStruct((27, 16, 256), f32),
         ),
-        in_specs=[vmem] * 3,
+        in_specs=[pl.BlockSpec(memory_space=pltpu.HBM)] * 3,
         out_specs=(vmem,) * 3,
         scratch_shapes=[
+            pltpu.VMEM((2, 2, 16, 8, 128), bf16),
+            pltpu.VMEM((27, 16, 256), bf16),
             pltpu.VMEM((2, 128, 128), f32),
             pltpu.VMEM((2, 16, 1024), bf16),
             pltpu.VMEM((2, 16, 1024), bf16),
@@ -475,19 +493,21 @@
             pltpu.SemaphoreType.DMA((COPIES,)),
             pltpu.SemaphoreType.DMA((COPIES,)),
             pltpu.SemaphoreType.REGULAR((2,)),
+            pltpu.SemaphoreType.DMA((3,)),
         ],
         compiler_params=pltpu.CompilerParams(
-            collective_id=0, has_side_effects=True, vmem_limit_bytes=48 << 20
+            collective_id=0, has_side_effects=True, vmem_limit_bytes=61 << 20
         ),
         name="layer",
     )(volume, cotangent, kernel)
     return pl.pallas_call(
         store_kernel,
         out_shape=tuple(jax.ShapeDtypeStruct(x.shape, x.dtype) for x in results),
-        in_specs=[vmem] * 3,
+        in_specs=[pl.BlockSpec(memory_space=pltpu.HBM)] * 3,
         out_specs=(pl.BlockSpec(memory_space=pltpu.HBM),) * 3,
-        scratch_shapes=[pltpu.SemaphoreType.DMA((3,))],
-        compiler_params=pltpu.CompilerParams(vmem_limit_bytes=8 << 20),
+        scratch_shapes=[pltpu.VMEM(x.shape, x.dtype) for x in results]
+        + [pltpu.SemaphoreType.DMA((6,))],
+        compiler_params=pltpu.CompilerParams(vmem_limit_bytes=61 << 20),
         name="store",
     )(*results)
 

time: 53.9 us -> 53.1 us (0.985)
  local copies, waits for them, and re-layouts: 2.61 us -> 0 us
  Pallas kernels: 50.4 us -> 52.3 us
    unnamed x6 -> x0, local copies, waits for them, and re-layouts: 2.61 us -> none
    pallas_call x1, Pallas kernels: 0.82 us -> 1.86 us  [on_device(): pl.pallas_call(store_kernel, out_shape=tuple((jax.ShapeDtypeStruct(x.shap...]
    pallas_call x1, Pallas kernels: 49.6 us -> 50.4 us  [on_device(): pl.pallas_call(functools.partial(layer_kernel, nspace, scale), out_shape=...]
where the time goes in v7:
time: 53.1 us; the launch traced here: 52.9 us
  Pallas kernels  52.3 us (98%)
  between operations  0.64 us (1%)
    pallas_call x1, Pallas kernels, on_device(): pl.pallas_call(functools.partial(layer_kernel, nspace, scale), out_shape=...  50.4 us
    pallas_call x1, Pallas kernels, on_device(): pl.pallas_call(store_kernel, out_shape=tuple((jax.ShapeDtypeStruct(x.shap...  1.86 us

profile of v7, /device:TPU:1, one launch (start us, length us, event | category | flops | bytes accessed | tf_op | source)
XLA Modules:
  0.0 52.9 jit_solution(6647190489860509729)
XLA Ops:
  0.6 50.4 %layer.1 = (bf16[2,16,8,128]{3,2,1,0:T(8,128)(2,1)}, bf16[2,16,8,128]{3,2,1,0:T(8,128)(2,1)}, f32[27,16,256]{2,1,0:T(8,128)}) custom-call(bf16[2,16,8,128]{3,2,1,0:T(8,128)(2,1)} %vol_hbm.1, bf16[2,16,8,128]{3,2,1,0:T(8,128)(2,1)} %cot_hbm.1, bf16[27,16,256]{2,1,0:T(8,128)(2,1)} %ker_hbm.1), custom_call_target="tpu_custom_call" | custom-call | tf_op jit(solution)/shard_map/layer/pallas_call | solution.py:465
  51.0 1.9 %store.1 = (bf16[2,16,8,128]{3,2,1,0:T(8,128)(2,1)}, bf16[2,16,8,128]{3,2,1,0:T(8,128)(2,1)}, f32[27,16,256]{2,1,0:T(8,128)}) custom-call(bf16[2,16,8,128]{3,2,1,0:T(8,128)(2,1)} %get-tuple-element.6.a_ref, bf16[2,16,8,128]{3,2,1,0:T(8,128)(2,1)} %get-tuple-element.7.b_ref, f32[27,16,256]{2,1,0:T(8,128)} %get-tuple-element.8.c_ref), custom_call_target="tpu_custom_call" | custom-call | tf_op jit(solution)/shard_map/store/pallas_call | solution.py:503
